TPU v7x, 32 devices: a whole 2x2x4 slice. The times are simulated.
32 devices in a mesh: ty: 4 (over y, x), tx: 4 (over z), slide: 2 (over core).
Axes of the slice: x: 2, y: 2, z: 4, core: 2. Of those that a mesh axis runs over, the one named last changes fastest.
Arguments:
- tokens: bfloat16 [8, 4, 192, 768], P(('slide', 'ty'), 'tx'), parts along dimension 0, may hold values from -6 to 6
- summary: bfloat16 [512, 768], P(('slide', 'ty', 'tx')), parts along dimension 0, may hold values from -6 to 6
- counts: int32 [8, 4], P('slide'), parts along dimension 0, may hold values from 1 to 192, as said below
- tile_pattern: int32 [8, 4, 9], P('slide'), parts along dimension 0, may hold values from 0 to 1, as said below
- summary_pattern: int32 [8, 4, 2], P(('slide', 'ty'), 'tx'), parts along dimension 0, may hold values 0 or 1
- norm_gain: float32 [768], replicated, may hold values from 0.1 to 1.9
- projections: bfloat16 [4, 768, 768], replicated, may hold values from -4 to 4
- cotangent: bfloat16 [8, 4, 192, 768], P(('slide', 'ty'), 'tx'), parts along dimension 0, may hold values from -6 to 6
Outputs:
- updated: bfloat16 [8, 4, 192, 768], P(('slide', 'ty'), 'tx'), parts along dimension 0
- grad_tokens: bfloat16 [8, 4, 192, 768], P(('slide', 'ty'), 'tx'), parts along dimension 0
- grad_summary: bfloat16 [512, 768], P(('slide', 'ty', 'tx')), parts along dimension 0
- grad_proj: float32 [8, 768, 768], P('slide'), parts along dimension 0
- grad_gain: float32 [1536], P('slide'), parts along dimension 0
There are 2 independent parts, one for each index of `slide`. A program takes and returns all parts, laid end to end along the dimension named above; an argument that names none is the same for every part. Nothing has to cross between parts.
Inputs may be any that keep to these rules, and one draw needn't show every extreme that they name: `counts`: some tile holds exactly 192 tokens and some tile exactly 1 in every draw. `tile_pattern`: entry 4, the tile itself, is always 1.
All inputs are finite; a program needn't handle non-finite values. No bound on the sum of `summary_pattern` on one device may be relied on, other than what follows from the above.
Results may differ from a plain program's by a relative error of at most 0.011.
Values may be sent and summed in bfloat16 or wider, within the bound.
No kernel may reach another device: no remote copies, remote signals or barrier semaphores. Data moves between devices by JAX's collectives and lax.ppermute only.
A program may use at most 128 MiB of HBM per device.

v0:
```python
import functools
import math

import jax
import jax.numpy as jnp
from jax import lax
from jax.experimental import pallas as pl
from jax.experimental.pallas import tpu as pltpu
from jax.sharding import PartitionSpec as P


HEADS = 12
SBLK = 128
CHUNK = 256
BLOCK = 512
GROUP = 16
FAR = -1e30
epsilon = 1e-05


f32 = jnp.float32
bf16 = jnp.bfloat16


def shifted(array, axis, by):
    peers = lax.axis_size(axis)
    pairs = [(i, i + by) for i in range(peers) if 0 <= i + by < peers]
    return lax.ppermute(array, axis, pairs)


def rotated(array, axis, by):
    peers = lax.axis_size(axis)
    return lax.ppermute(array, axis, [(i, (i + by) % peers) for i in range(peers)])


def swapped(array, axis, bit):
    peers = lax.axis_size(axis)
    return lax.ppermute(array, axis, [(i, i ^ (1 << bit)) for i in range(peers)])


def rms_scale(rows):
    values = rows.astype(f32)
    return lax.rsqrt(jnp.mean(values * values, axis=-1, keepdims=True) + epsilon)


def norm_back(rows, scale, gain, grad_norm):
    values = rows.astype(f32)
    scaled = gain * grad_norm
    return scale * scaled - values * scale**3 * jnp.mean(values * scaled, axis=-1, keepdims=True)


def mm(left, right, contract=((1,), (0,))):
    return lax.dot_general(left, right, (contract, ((), ())), preferred_element_type=f32)


def layer_kernel(segments, n_in, meta, tokens, query, grad, masked, weights, *refs):
    sources = refs[:n_in]
    outs = refs[n_in:]
    updated_ref, dw_ref = outs[:2]
    targets = outs[2 : 2 + n_in]
    (hc, hct, bias, k_s, v_s, e_s, acc_s, o_s, dq_s, dw_s) = outs[2 + n_in :]
    own_ref = sources[0]
    n_seg = len(segments)
    rows = own_ref.shape[0]
    width = own_ref.shape[1]
    half = width // HEADS
    pairs = HEADS // 2
    lanes = 2 * rows
    factor = 1.0 / math.sqrt(half)
    total = meta[0, n_seg]
    chunks = lax.div(total + (CHUNK - 1), CHUNK)
    blocks = lax.div(total + (BLOCK - 1), BLOCK)
    own_count = meta[1, n_seg]

    offset = jnp.int32(0)
    for s, (which, start) in enumerate(segments):
        valid = meta[1, s]

        def gather(j, carry, which=which, start=start, valid=valid, offset=offset):
            there = pl.multiple_of(offset + j * GROUP, GROUP)
            here = pl.multiple_of(start + j * GROUP, GROUP)
            hc[pl.ds(there, GROUP), :] = sources[which][pl.ds(here, GROUP), :]
            place = lax.broadcasted_iota(jnp.int32, (GROUP, 128), 0) + j * GROUP
            bias[pl.ds(there, GROUP), :] = jnp.where(place < valid, 0.0, FAR)
            return carry

        lax.fori_loop(0, meta[0, s], gather, 0)
        offset = offset + meta[0, s] * GROUP

    def tail(j, carry):
        there = pl.multiple_of(j * GROUP, GROUP)
        hc[pl.ds(there, GROUP), :] = jnp.zeros((GROUP, width), bf16)
        bias[pl.ds(there, GROUP), :] = jnp.full((GROUP, 128), FAR, f32)
        return carry

    lax.fori_loop(lax.div(total, GROUP), blocks * (BLOCK // GROUP), tail, 0)

    def block_at(c):
        return pl.ds(pl.multiple_of(c * BLOCK, BLOCK), BLOCK)

    def chunk_at(c):
        return pl.ds(pl.multiple_of(c * CHUNK, CHUNK), CHUNK)

    def project(c, carry):
        at = block_at(c)
        h = hc[at, :]
        hct[c] = h.T
        for n in range(0, width, 256):
            k_s[at, n : n + 256] = mm(h, weights[1, :, n : n + 256]).astype(bf16)
            v_s[at, n : n + 256] = mm(h, weights[2, :, n : n + 256]).astype(bf16)
        return carry

    lax.fori_loop(0, blocks, project, 0)

    low = lax.broadcasted_iota(jnp.int32, (rows, 128), 1) < half

    def two(ref, i):
        part = ref[:, 128 * i : 128 * (i + 1)]
        nil = jnp.zeros_like(part)
        return jnp.concatenate([jnp.where(low, part, nil), jnp.where(low, nil, part)], axis=0)

    def merged(stacked_t):
        stacked = stacked_t.T
        return jnp.where(low, stacked[:rows], stacked[rows:])

    def score(i, c, q2t, largest):
        at = chunk_at(c)
        b = bias[at, :]
        scores = mm(k_s[at, 128 * i : 128 * (i + 1)], q2t)
        scores = scores + jnp.concatenate([b] * (lanes // 128), axis=1)
        e_s[i % 2, at, :] = scores
        return jnp.maximum(largest, jnp.max(scores.reshape(CHUNK // 8, 8, lanes), axis=0))

    nothing = jnp.full((8, lanes), FAR, f32)
    q2t = two(query, 0).T
    largest = lax.fori_loop(0, chunks, lambda c, m: score(0, c, q2t, m), nothing)

    for i in range(pairs):
        q2 = two(query, i)
        g2 = two(grad, i)
        g2t = g2.T
        cols = slice(128 * i, 128 * (i + 1))
        top = jnp.max(largest, axis=0, keepdims=True)
        acc_s[...] = jnp.zeros_like(acc_s)

        def weigh(c, sums):
            at = chunk_at(c)
            e = jnp.exp(e_s[i % 2, at, :] - top)
            e_s[i % 2, at, :] = e
            acc_s[...] += mm(v_s[at, cols], e.astype(bf16), ((0,), (0,)))
            return sums + jnp.sum(e.reshape(CHUNK // 8, 8, lanes), axis=0)

        sums = lax.fori_loop(0, chunks, weigh, jnp.zeros((8, lanes), f32))
        inverse = 1.0 / jnp.sum(sums, axis=0, keepdims=True)
        out_t = acc_s[...] * inverse
        delta = jnp.sum(g2t.astype(f32) * out_t, axis=0, keepdims=True)
        o_s[:, cols] = merged(out_t).astype(bf16)
        acc_s[...] = jnp.zeros_like(acc_s)
        more = i + 1 < pairs
        if more:
            q2t = two(query, i + 1).T

        def back(c, largest):
            at = chunk_at(c)
            if more:
                largest = score(i + 1, c, q2t, largest)
            probs = e_s[i % 2, at, :] * inverse
            dscore = (probs * (mm(v_s[at, cols], g2t) - delta)).astype(bf16)
            acc_s[...] += mm(k_s[at, cols], dscore, ((0,), (0,)))
            k_s[at, cols] = mm(dscore, q2).astype(bf16)
            v_s[at, cols] = mm(probs.astype(bf16), g2).astype(bf16)
            return largest

        largest = lax.fori_loop(0, chunks, back, nothing)
        dq_s[:, cols] = (merged(acc_s[...]) * factor).astype(bf16)

    own_t = own_ref[...].T
    attended = o_s[...]
    attended_t = attended.T
    dquery = dq_s[...]
    live = lax.broadcasted_iota(jnp.int32, (rows, 256), 0) < own_count
    for n in range(0, width, 256):
        cut = slice(n, n + 256)
        moved = jnp.where(live, mm(attended, weights[3, :, cut]), 0.0)
        updated_ref[:, cut] = (tokens[:, cut].astype(f32) + moved).astype(bf16)
        dw_ref[0, :, cut] = mm(own_t, dquery[:, cut]).astype(bf16)
        dw_ref[3, :, cut] = mm(attended_t, masked[:, cut]).astype(bf16)
        targets[0][:, cut] = mm(dquery, weights[0, cut, :], ((1,), (1,)))
    for source, into in ((k_s, 1), (v_s, 2)):

        def outer(c, carry, source=source, into=into):
            at = block_at(c)
            for n in range(0, width, 256):
                dw_s[:, n : n + 256] += mm(hct[c], source[at, n : n + 256])
            return carry

        dw_s[...] = jnp.zeros_like(dw_s)
        lax.fori_loop(0, blocks, outer, 0)
        dw_ref[into] = dw_s[...].astype(bf16)

    def returned(c, carry):
        at = block_at(c)
        for n in range(0, width, 256):
            cut = slice(n, n + 256)
            hc[at, cut] = (
                mm(k_s[at, :], weights[1, cut, :], ((1,), (1,)))
                + mm(v_s[at, :], weights[2, cut, :], ((1,), (1,)))
            ).astype(bf16)
        return carry

    lax.fori_loop(0, blocks, returned, 0)
    for target in targets[1:]:
        target[...] = jnp.zeros_like(target)
    offset = jnp.int32(0)
    for s, (which, start) in enumerate(segments):

        def scatter(j, carry, which=which, start=start, offset=offset):
            there = pl.multiple_of(offset + j * GROUP, GROUP)
            here = pl.multiple_of(start + j * GROUP, GROUP)
            part = hc[pl.ds(there, GROUP), :]
            if which == 0:
                targets[0][pl.ds(here, GROUP), :] += part.astype(f32)
            else:
                targets[which][pl.ds(here, GROUP), :] = part
            return carry

        lax.fori_loop(0, meta[0, s], scatter, 0)
        offset = offset + meta[0, s] * GROUP


def layer(meta, segments, tokens, query, grad, masked, sources, projections):
    rows, width = tokens.shape
    most = sum(a.shape[0] for a in sources)
    room = -(-most // BLOCK) * BLOCK
    vmem = pl.BlockSpec(memory_space=pltpu.VMEM)
    out_shape = [
        jax.ShapeDtypeStruct((rows, width), bf16),
        jax.ShapeDtypeStruct((4, width, width), bf16),
        jax.ShapeDtypeStruct((rows, width), f32),
    ] + [jax.ShapeDtypeStruct(a.shape, bf16) for a in sources[1:]]
    scratch = [
        pltpu.VMEM((room, width), bf16),
        pltpu.VMEM((room // BLOCK, width, BLOCK), bf16),
        pltpu.VMEM((room, 128), f32),
        pltpu.VMEM((room, width), bf16),
        pltpu.VMEM((room, width), bf16),
        pltpu.VMEM((2, room, 2 * rows), f32),
        pltpu.VMEM((128, 2 * rows), f32),
        pltpu.VMEM((rows, width), bf16),
        pltpu.VMEM((rows, width), bf16),
        pltpu.VMEM((width, width), f32),
    ]
    held = room * (3 * width * 2 + width * 2 + 512 + 16 * rows) + 6 * width * width * 4
    grant = held + 4 * most * width + 6 * 2**20
    return pl.pallas_call(
        functools.partial(layer_kernel, segments, len(sources)),
        in_specs=[pl.BlockSpec(memory_space=pltpu.SMEM)] + [vmem] * (5 + len(sources)),
        out_specs=[vmem] * len(out_shape),
        out_shape=out_shape,
        scratch_shapes=scratch,
        compiler_params=pltpu.CompilerParams(vmem_limit_bytes=grant),
        name="layer",
    )(meta, tokens, query, grad, masked, projections, *sources)


def half_of(array, index):
    size = array.shape[0] // 2
    return lax.dynamic_slice_in_dim(array, index * size, size, axis=0)


def added(left, right):
    return (left.astype(f32) + right.astype(f32)).astype(bf16)


def in_order(pieces, place):
    count = len(pieces)
    ring = jnp.stack([pieces[-m % count] for m in range(count)] * 2)
    return lax.dynamic_slice_in_dim(ring, (count - place) % count, count, axis=0)


def split_bits(peers):
    return [b for b in range(peers.bit_length() - 1)]


def fold(arrays, axis, b, place):
    mine = (place >> b) & 1
    sent = [half_of(a, 1 - mine) for a in arrays]
    got = swapped(sent[0] if len(sent) == 1 else jnp.concatenate(sent, axis=0), axis, b)
    kept, start = [], 0
    for a in arrays:
        size = a.shape[0] // 2
        kept.append(added(half_of(a, mine), got[start : start + size]))
        start += size
    return kept


def unfold(array, axis, b, place):
    other = swapped(array, axis, b)
    return jnp.where(
        ((place >> b) & 1) == 1,
        jnp.concatenate([other, array], axis=0),
        jnp.concatenate([array, other], axis=0),
    )


def fold_line(arrays, axis, place):
    peers = lax.axis_size(axis)

    def part(index):
        return jnp.concatenate(
            [
                lax.dynamic_slice_in_dim(
                    a, (index % peers) * (a.shape[0] // peers), a.shape[0] // peers, axis=0
                )
                for a in arrays
            ],
            axis=0,
        )

    got = [rotated(part(place + k), axis, k) for k in range(1, peers)]
    result = part(place).astype(f32)
    for g in got:
        result = result + g.astype(f32)
    return result


def after(value, *others):
    return lax.optimization_barrier((value,) + others)[0]


def local(
    tokens, summary, counts, tile_pattern, summary_pattern, norm_gain, projections, cotangent
):
    tile = tokens.shape[2]
    width = tokens.shape[3]
    n_ty = lax.axis_size("ty")
    n_tx = lax.axis_size("tx")
    row = lax.axis_index("ty")
    col = lax.axis_index("tx")
    zero = jnp.zeros((), jnp.int32)
    rows = tokens[0, 0]
    grads = cotangent[0, 0]
    row_scale = rms_scale(rows)
    hidden = (rows.astype(f32) * row_scale * norm_gain).astype(bf16)
    summary_scale = rms_scale(summary)
    summary_hidden = (summary.astype(f32) * summary_scale * norm_gain).astype(bf16)

    bits = split_bits(n_ty)
    back_bits = bits[::-1]
    gathered = summary_hidden
    for b in bits:
        gathered = unfold(gathered, "ty", b, row)
    up = shifted(hidden, "ty", 1)
    down = shifted(hidden, "ty", -1)
    left = shifted(hidden, "tx", 1)
    right = shifted(hidden, "tx", -1)
    columns = [gathered]
    for k in range(1, n_tx):
        columns.append(rotated(gathered, "tx", k))
    both = jnp.concatenate([up, down], axis=0)
    left_two = shifted(both, "tx", 1)
    right_two = shifted(both, "tx", -1)
    each = summary.shape[0]
    every_summary = (
        in_order(columns, col)
        .reshape(n_tx, n_ty, each, width)
        .transpose(1, 0, 2, 3)
        .reshape(n_ty * n_tx * each, width)
    )

    live = jnp.arange(tile, dtype=jnp.int32)[:, None] < lax.dynamic_slice(
        counts, (row, col), (1, 1)
    )
    masked = jnp.where(live, grads, jnp.zeros_like(grads))
    factor = 1.0 / math.sqrt(width // HEADS)
    query = (mm(hidden, projections[0]).astype(bf16) * factor).astype(bf16)
    grad = mm(masked, projections[3], ((1,), (1,))).astype(bf16)
    near_counts = lax.dynamic_slice(jnp.pad(counts, 1), (row, col), (3, 3)).reshape(9)
    flags = lax.dynamic_slice(tile_pattern, (row, col, zero), (1, 1, 9)).reshape(9)
    valid = jnp.concatenate(
        [
            jnp.where(flags == 1, near_counts, 0),
            jnp.where(summary_pattern[0, 0] == 1, SBLK, 0),
        ]
    ).astype(jnp.int32)
    groups = (valid + GROUP - 1) // GROUP
    meta = jnp.stack(
        [
            jnp.concatenate([groups, jnp.sum(groups, keepdims=True) * GROUP]),
            jnp.concatenate([valid, near_counts[4:5]]),
        ]
    ).astype(jnp.int32)
    segments = (
        (5, 0), (1, 0), (6, 0),
        (3, 0), (0, 0), (4, 0),
        (5, tile), (2, 0), (6, tile),
    ) + tuple((7, SBLK * b) for b in range(summary_pattern.shape[2]))
    sources = [hidden, up, down, left, right, left_two, right_two, every_summary]
    results = layer(meta, segments, rows, query, grad, masked, sources, projections)
    updated, dw = results[:2]
    d_own, d_up, d_down, d_left, d_right, d_left_two, d_right_two, d_summary = results[2:]

    def halves(left_list, right_list, level):
        return (
            fold(left_list, "ty", bits[level], row),
            fold(right_list, "ty", back_bits[level], row),
        )

    one = ([dw[0]], [dw[3]])
    one = halves(*one, 0)
    far_right = shifted(d_right_two, "tx", 1)
    far_left = shifted(d_left_two, "tx", -1)
    from_left = shifted(d_right, "tx", 1)
    from_right = shifted(d_left, "tx", -1)
    two = ([after(dw[1], *one[0])], [after(dw[2], *one[1]), d_summary])
    two = halves(*two, 0)
    for level in range(1, len(bits)):
        one = halves(*one, level)
    for level in range(1, len(bits)):
        two = halves(*two, level)
    one = fold_line(one[0] + one[1], "tx", col).astype(bf16)
    pair_sum = (
        jnp.concatenate([d_up, d_down], axis=0).astype(f32)
        + far_right.astype(f32)
        + far_left.astype(f32)
    ).astype(bf16)
    pair_sum = after(pair_sum, *two[0])
    from_above = shifted(pair_sum[tile:], "ty", 1)
    from_below = shifted(pair_sum[:tile], "ty", -1)
    hidden_grad = (
        d_own
        + from_left.astype(f32)
        + from_right.astype(f32)
        + from_above.astype(f32)
        + from_below.astype(f32)
    )
    two = fold_line(two[0] + two[1], "tx", col)
    summary_hidden_grad = two[-each:]
    two = two[:-each].astype(bf16)

    def spread(block):
        pieces = [block] + [rotated(block, "tx", k) for k in range(1, n_tx)]
        stacked = in_order(pieces, col)
        size = block.shape[0] // 2
        a = stacked[:, :size].reshape(n_tx * size, width)
        b = stacked[:, size:].reshape(n_tx * size, width)
        for level in reversed(range(len(bits))):
            a = unfold(a, "ty", bits[level], row)
            b = unfold(b, "ty", back_bits[level], row)
        return a, b

    g_query, g_out = spread(one)
    g_key, g_value = spread(two)
    grad_proj = jnp.stack([g_query, g_key, g_value, g_out]).astype(f32)
    grad_gain = jnp.sum(grad_proj[:3] * projections[:3].astype(f32), axis=(0, 2)) / norm_gain
    grad_tokens = (
        grads.astype(f32) + norm_back(rows, row_scale, norm_gain, hidden_grad)
    ).astype(bf16)
    grad_summary = norm_back(summary, summary_scale, norm_gain, summary_hidden_grad).astype(bf16)
    return (
        updated.reshape(tokens.shape),
        grad_tokens.reshape(tokens.shape),
        grad_summary,
        grad_proj,
        grad_gain,
    )


def solution(mesh):
    return jax.shard_map(
        local,
        mesh=mesh,
        in_specs=(
            P(("slide", "ty"), "tx", None, None),
            P(("slide", "ty", "tx"), None),
            P("slide", None),
            P("slide", None, None),
            P(("slide", "ty"), "tx", None),
            P(),
            P(),
            P(("slide", "ty"), "tx", None, None),
        ),
        out_specs=(
            P(("slide", "ty"), "tx", None, None),
            P(("slide", "ty"), "tx", None, None),
            P(("slide", "ty", "tx"), None),
            P("slide", None, None),
            P("slide"),
        ),
        check_vma=False,
    )
```

profile of v0, /device:TPU:0, one launch (start us, length us, event | category | flops | bytes accessed | tf_op | source)
XLA Modules:
  0.0 257.9 jit_solution(407710140809305657)
XLA Ops:
  4.2 5.6 %collective-permute-start.2 = (bf16[192,768]{1,0:T(8,128)(2,1)S(1)}, bf16[192,768]{1,0:T(8,128)(2,1)S(1)}, u32[]{:S(2)}, u32[]{:S(2)}) collective-permute-start(bf16[192,768]{1,0:T(8,128)(2,1)S(1)} %fusion.12.refs_0_), channel_id=1, source_target_pairs={{0,2},{2,4},{4,6},{1,3},{3,5},{5,7},{8,10},{10,12},{12,14},{9,11},... | collective-permute-start | bytes 884744 | tf_op jit(solution)/shard_map/ppermute | solution.py:28
  11.1 4.6 %collective-permute-start = (bf16[192,768]{1,0:T(8,128)(2,1)S(1)}, bf16[192,768]{1,0:T(8,128)(2,1)S(1)}, u32[]{:S(2)}, u32[]{:S(2)}) collective-permute-start(bf16[192,768]{1,0:T(8,128)(2,1)S(1)} %fusion.12.refs_0_), channel_id=1, source_target_pairs={{0,8},{8,16},{16,24},{1,9},{9,17},{17,25},{2,10},{10,18},{18,26},{... | collective-permute-start | bytes 884744 | tf_op jit(solution)/shard_map/ppermute | solution.py:28
  17.3 2.8 %collective-permute-start.6 = (bf16[16,768]{1,0:T(8,128)(2,1)S(1)}, bf16[16,768]{1,0:T(8,128)(2,1)S(1)}, u32[]{:S(2)}, u32[]{:S(2)}) collective-permute-start(bf16[16,768]{1,0:T(8,128)(2,1)S(1)} %fusion.29), channel_id=1, source_target_pairs={{0,8},{8,0},{16,24},{24,16},{1,9},{9,1},{17,25},{25,17},{2,10},{10... | collective-permute-start | bytes 73736 | tf_op jit(solution)/shard_map/ppermute | solution.py:38
  22.1 2.6 %fusion.7.query = bf16[192,768]{1,0:T(8,128)(2,1)} fusion(bf16[4,768,768]{2,1,0:T(8,128)(2,1)} %weights.1, bf16[1,1,192,768]{3,2,1,0:T(8,128)(2,1)} %param.8, f32[768]{0:T(1024)} %param.13, f32[192]{0:T(256)S(1)} %get-tuple-element.70), kind=kOutput, calls=%fused_computation.22 | convolution fusion | flops 227377152 | bytes 1774336 | tf_op jit(solution)/shard_map/dot_general | solution.py:53
  24.8 2.6 convolution_convert_fusion.grad
  31.1 4.0 %collective-permute-done.7 = bf16[32,768]{1,0:T(8,128)(2,1)S(1)} collective-permute-done((bf16[32,768]{1,0:T(8,128)(2,1)S(1)}, bf16[32,768]{1,0:T(8,128)(2,1)S(1)}, u32[]{:S(2)}, u32[]{:S(2)}) %collective-permute-start.7) | collective-permute-done | bytes 49184 | tf_op jit(solution)/shard_map/ppermute | solution.py:38
  36.6 3.8 %collective-permute-done.8 = bf16[64,768]{1,0:T(8,128)(2,1)S(1)} collective-permute-done((bf16[64,768]{1,0:T(8,128)(2,1)S(1)}, bf16[64,768]{1,0:T(8,128)(2,1)S(1)}, u32[]{:S(2)}, u32[]{:S(2)}) %collective-permute-start.8) | collective-permute-done | bytes 98336 | tf_op jit(solution)/shard_map/ppermute | solution.py:33
  40.5 2.6 %collective-permute-start.9 = (bf16[64,768]{1,0:T(8,128)(2,1)S(1)}, bf16[64,768]{1,0:T(8,128)(2,1)S(1)}, u32[]{:S(2)}, u32[]{:S(2)}) collective-permute-start(bf16[64,768]{1,0:T(8,128)(2,1)S(1)} %maximum_select_fusion.9), channel_id=1, source_target_pairs={{0,4},{2,6},{4,0},{6,2},{1,5},{3,7},{5,1},{7,3},{8,12},{10,14},{12... | collective-permute-start | bytes 294920 | tf_op jit(solution)/shard_map/ppermute | solution.py:33
  43.1 2.9 %collective-permute-done.9 = bf16[64,768]{1,0:T(8,128)(2,1)S(1)} collective-permute-done((bf16[64,768]{1,0:T(8,128)(2,1)S(1)}, bf16[64,768]{1,0:T(8,128)(2,1)S(1)}, u32[]{:S(2)}, u32[]{:S(2)}) %collective-permute-start.9) | collective-permute-done | bytes 98336 | tf_op jit(solution)/shard_map/ppermute | solution.py:33
  46.0 3.2 %collective-permute-start.10 = (bf16[64,768]{1,0:T(8,128)(2,1)S(1)}, bf16[64,768]{1,0:T(8,128)(2,1)S(1)}, u32[]{:S(2)}, u32[]{:S(2)}) collective-permute-start(bf16[64,768]{1,0:T(8,128)(2,1)S(1)} %maximum_select_fusion.9), channel_id=1, source_target_pairs={{0,2},{2,4},{4,6},{6,0},{1,3},{3,5},{5,7},{7,1},{8,10},{10,12},{12... | collective-permute-start | bytes 294920 | tf_op jit(solution)/shard_map/ppermute | solution.py:33
  49.2 3.6 %collective-permute-done.10 = bf16[64,768]{1,0:T(8,128)(2,1)S(1)} collective-permute-done((bf16[64,768]{1,0:T(8,128)(2,1)S(1)}, bf16[64,768]{1,0:T(8,128)(2,1)S(1)}, u32[]{:S(2)}, u32[]{:S(2)}) %collective-permute-start.10) | collective-permute-done | bytes 98336 | tf_op jit(solution)/shard_map/ppermute | solution.py:33
  54.3 4.6 %collective-permute-start.4 = (bf16[384,768]{1,0:T(8,128)(2,1)S(1)}, bf16[384,768]{1,0:T(8,128)(2,1)S(1)}, u32[]{:S(2)}, u32[]{:S(2)}) collective-permute-start(bf16[384,768]{1,0:T(8,128)(2,1)S(1)} %constant_dynamic-update-slice_fusion), channel_id=1, source_target_pairs={{0,2},{2,4},{4,6},{1,3},{3,5},{5,7},{8,10},{10,12},{12,14},{9,11},... | collective-permute-start | bytes 1769480 | tf_op jit(solution)/shard_map/ppermute | solution.py:28
  59.8 5.5 %collective-permute-done.5.refs_6_ = bf16[384,768]{1,0:T(8,128)(2,1)S(1)} collective-permute-done((bf16[384,768]{1,0:T(8,128)(2,1)S(1)}, bf16[384,768]{1,0:T(8,128)(2,1)S(1)}, u32[]{:S(2)}, u32[]{:S(2)}) %collective-permute-start.5) | collective-permute-done | bytes 589856 | tf_op jit(solution)/shard_map/ppermute | solution.py:28
  67.4 32.6 %layer.1 = (bf16[192,768]{1,0:T(8,128)(2,1)}, bf16[4,768,768]{2,1,0:T(8,128)(2,1)}, f32[192,768]{1,0:T(8,128)S(1)}, bf16[192,768]{1,0:T(8,128)(2,1)S(1)}, bf16[1...) custom-call(s32[2,12]{1,0:T(2,128)S(1)} %pad_add_fusion.meta, ...), custom_call_target="tpu_custom_call" | custom-call | tf_op jit(solution)/shard_map/layer/pallas_call | solution.py:255
  100.0 4.9 %fusion.37 = (bf16[1,768,768]{2,1,0:T(8,128)(2,1)}, bf16[768,768]{1,0:T(8,128)(2,1)}, bf16[1,768,768]{2,1,0:T(8,128)(2,1)S(1)}, bf16[768,768]{1,0:T(8,128)(2,1)}) fusion(bf16[4,768,768]{2,1,0:T(8,128)(2,1)} %get-tuple-element.26), kind=kLoop, calls=%fused_computation.165 | loop fusion | bytes 9437184 | tf_op jit(solution)/shard_map/slice | solution.py:409
  106.8 5.9 %collective-permute-start.15 = (bf16[384,768]{1,0:T(8,128)(2,1)}, bf16[384,768]{1,0:T(8,128)(2,1)}, u32[]{:S(2)}, u32[]{:S(2)}) collective-permute-start(bf16[384,768]{1,0:T(8,128)(2,1)} %dynamic-slice_bitcast_fusion.1), channel_id=1, source_target_pairs={{0,8},{8,0},{16,24},{24,16},{1,9},{9,1},{17,25},{25,17},{2,10},{10... | collective-permute-start | bytes 1769480 | tf_op jit(solution)/shard_map/ppermute | solution.py:38
  112.6 4.4 %collective-permute-start.11 = (bf16[192,768]{1,0:T(8,128)(2,1)}, bf16[192,768]{1,0:T(8,128)(2,1)S(1)}, u32[]{:S(2)}, u32[]{:S(2)}) collective-permute-start(bf16[192,768]{1,0:T(8,128)(2,1)} %copy-done.11), channel_id=1, source_target_pairs={{0,2},{2,4},{4,6},{1,3},{3,5},{5,7},{8,10},{10,12},{12,14},{9,11},... | collective-permute-start | bytes 884744 | tf_op jit(solution)/shard_map/ppermute | solution.py:28
  121.4 14.5 %collective-permute-start.20 = (bf16[384,768]{1,0:T(8,128)(2,1)S(1)}, bf16[384,768]{1,0:T(8,128)(2,1)S(1)}, u32[]{:S(2)}, u32[]{:S(2)}) collective-permute-start(bf16[384,768]{1,0:T(8,128)(2,1)S(1)} %dynamic-slice_bitcast_fusion), channel_id=1, source_target_pairs={{0,16},{8,24},{16,0},{24,8},{1,17},{9,25},{17,1},{25,9},{2,18},{10... | collective-permute-start | bytes 1769480 | tf_op jit(solution)/shard_map/ppermute | solution.py:38
  137.5 6.3 %collective-permute-done.20 = bf16[384,768]{1,0:T(8,128)(2,1)S(1)} collective-permute-done((bf16[384,768]{1,0:T(8,128)(2,1)S(1)}, bf16[384,768]{1,0:T(8,128)(2,1)S(1)}, u32[]{:S(2)}, u32[]{:S(2)}) %collective-permute-start.20) | collective-permute-done | bytes 589856 | tf_op jit(solution)/shard_map/ppermute | solution.py:38
  147.1 9.7 %collective-permute-done.27 = bf16[192,768]{1,0:T(8,128)(2,1)S(1)} collective-permute-done((bf16[192,768]{1,0:T(8,128)(2,1)S(1)}, bf16[192,768]{1,0:T(8,128)(2,1)S(1)}, u32[]{:S(2)}, u32[]{:S(2)}) %collective-permute-start.27) | collective-permute-done | bytes 294944 | tf_op jit(solution)/shard_map/ppermute | solution.py:38
  157.0 3.3 %collective-permute-start.28 = (bf16[96,768]{1,0:T(8,128)(2,1)S(1)}, bf16[96,768]{1,0:T(8,128)(2,1)S(1)}, u32[]{:S(2)}, u32[]{:S(2)}) collective-permute-start(bf16[96,768]{1,0:T(8,128)(2,1)S(1)} %pad_maximum_fusion.5), channel_id=1, source_target_pairs={{0,2},{2,4},{4,6},{6,0},{1,3},{3,5},{5,7},{7,1},{8,10},{10,12},{12... | collective-permute-start | bytes 442376 | tf_op jit(solution)/shard_map/ppermute | solution.py:33
  162.9 2.7 %collective-permute-done.28 = bf16[96,768]{1,0:T(8,128)(2,1)S(1)} collective-permute-done((bf16[96,768]{1,0:T(8,128)(2,1)S(1)}, bf16[96,768]{1,0:T(8,128)(2,1)S(1)}, u32[]{:S(2)}, u32[]{:S(2)}) %collective-permute-start.28) | collective-permute-done | bytes 147488 | tf_op jit(solution)/shard_map/ppermute | solution.py:33
  172.1 3.4 %collective-permute-start.31 = (bf16[96,768]{1,0:T(8,128)(2,1)S(1)}, bf16[96,768]{1,0:T(8,128)(2,1)S(1)}, u32[]{:S(2)}, u32[]{:S(2)}) collective-permute-start(bf16[96,768]{1,0:T(8,128)(2,1)S(1)} %get-tuple-element.34), channel_id=1, source_target_pairs={{0,6},{2,0},{4,2},{6,4},{1,7},{3,1},{5,3},{7,5},{8,14},{10,8},{12,... | collective-permute-start | bytes 442376 | tf_op jit(solution)/shard_map/ppermute | solution.py:33
  178.2 4.3 %collective-permute-start.32 = (bf16[96,768]{1,0:T(8,128)(2,1)S(1)}, bf16[96,768]{1,0:T(8,128)(2,1)S(1)}, u32[]{:S(2)}, u32[]{:S(2)}) collective-permute-start(bf16[96,768]{1,0:T(8,128)(2,1)S(1)} %get-tuple-element.34), channel_id=1, source_target_pairs={{0,4},{2,6},{4,0},{6,2},{1,5},{3,7},{5,1},{7,3},{8,12},{10,14},{12... | collective-permute-start | bytes 442376 | tf_op jit(solution)/shard_map/ppermute | solution.py:33
  182.5 4.6 %collective-permute-done.32 = bf16[96,768]{1,0:T(8,128)(2,1)S(1)} collective-permute-done((bf16[96,768]{1,0:T(8,128)(2,1)S(1)}, bf16[96,768]{1,0:T(8,128)(2,1)S(1)}, u32[]{:S(2)}, u32[]{:S(2)}) %collective-permute-start.32) | collective-permute-done | bytes 147488 | tf_op jit(solution)/shard_map/ppermute | solution.py:33
  191.2 5.9 %collective-permute-done.17 = bf16[192,768]{1,0:T(8,128)(2,1)S(1)} collective-permute-done((bf16[192,768]{1,0:T(8,128)(2,1)S(1)}, bf16[192,768]{1,0:T(8,128)(2,1)S(1)}, u32[]{:S(2)}, u32[]{:S(2)}) %collective-permute-start.17) | collective-permute-done | bytes 294944 | tf_op jit(solution)/shard_map/ppermute | solution.py:38
  216.5 2.7 %collective-permute-done.24 = bf16[112,768]{1,0:T(8,128)(2,1)S(1)} collective-permute-done((bf16[112,768]{1,0:T(8,128)(2,1)S(1)}, bf16[112,768]{1,0:T(8,128)(2,1)S(1)}, u32[]{:S(2)}, u32[]{:S(2)}) %collective-permute-start.24) | collective-permute-done | bytes 172064 | tf_op jit(solution)/shard_map/ppermute | solution.py:33
  219.3 2.9 %collective-permute-start.36 = (bf16[96,768]{1,0:T(8,128)(2,1)S(1)}, bf16[96,768]{1,0:T(8,128)(2,1)S(1)}, u32[]{:S(2)}, u32[]{:S(2)}) collective-permute-start(bf16[96,768]{1,0:T(8,128)(2,1)S(1)} %get-tuple-element.32), channel_id=1, source_target_pairs={{0,6},{2,0},{4,2},{6,4},{1,7},{3,1},{5,3},{7,5},{8,14},{10,8},{12,... | collective-permute-start | bytes 442376 | tf_op jit(solution)/shard_map/ppermute | solution.py:33
  224.9 6.5 %collective-permute-done.37 = bf16[96,768]{1,0:T(8,128)(2,1)S(1)} collective-permute-done((bf16[96,768]{1,0:T(8,128)(2,1)S(1)}, bf16[96,768]{1,0:T(8,128)(2,1)S(1)}, u32[]{:S(2)}, u32[]{:S(2)}) %collective-permute-start.37) | collective-permute-done | bytes 147488 | tf_op jit(solution)/shard_map/ppermute | solution.py:33
  234.7 3.6 %collective-permute-done.39 = bf16[192,768]{1,0:T(8,128)(2,1)S(1)} collective-permute-done((bf16[192,768]{1,0:T(8,128)(2,1)S(1)}, bf16[192,768]{1,0:T(8,128)(2,1)S(1)}, u32[]{:S(2)}, u32[]{:S(2)}) %collective-permute-start.39) | collective-permute-done | bytes 294944 | tf_op jit(solution)/shard_map/ppermute | solution.py:38
  242.9 5.9 %collective-permute-done.40 = bf16[384,768]{1,0:T(8,128)(2,1)S(1)} collective-permute-done((bf16[384,768]{1,0:T(8,128)(2,1)S(1)}, bf16[384,768]{1,0:T(8,128)(2,1)S(1)}, u32[]{:S(2)}, u32[]{:S(2)}) %collective-permute-start.40) | collective-permute-done | bytes 589856 | tf_op jit(solution)/shard_map/ppermute | solution.py:38
  254.3 3.0 %copy-done.12 = f32[4,768,768]{2,1,0:T(8,128)} copy-done((f32[4,768,768]{2,1,0:T(8,128)}, f32[4,768,768]{2,1,0:T(8,128)S(1)}, u32[]{:S(2)}) %copy-start.12) | copy-done | bytes 9437208
  (217 shorter events, 80.3 us)
Async XLA Ops:
  2.9 56.2 %collective-permute-start.3 = (bf16[192,768]{1,0:T(8,128)(2,1)S(1)}, bf16[192,768]{1,0:T(8,128)(2,1)S(1)}, u32[]{:S(2)}, u32[]{:S(2)}) collective-permute-start(bf16[192,768]{1,0:T(8,128)(2,1)S(1)} %fusion.12.refs_0_), channel_id=1, source_target_pairs={{2,0},{4,2},{6,4},{3,1},{5,3},{7,5},{10,8},{12,10},{14,12},{11,9},... | collective-permute-start | bytes 884744 | tf_op jit(solution)/shard_map/ppermute | solution.py:28
  4.2 54.9 %collective-permute-start.2 = (bf16[192,768]{1,0:T(8,128)(2,1)S(1)}, bf16[192,768]{1,0:T(8,128)(2,1)S(1)}, u32[]{:S(2)}, u32[]{:S(2)}) collective-permute-start(bf16[192,768]{1,0:T(8,128)(2,1)S(1)} %fusion.12.refs_0_), channel_id=1, source_target_pairs={{0,2},{2,4},{4,6},{1,3},{3,5},{5,7},{8,10},{10,12},{12,14},{9,11},... | collective-permute-start | bytes 884744 | tf_op jit(solution)/shard_map/ppermute | solution.py:28
  9.8 43.1 %collective-permute-start.1 = (bf16[192,768]{1,0:T(8,128)(2,1)S(1)}, bf16[192,768]{1,0:T(8,128)(2,1)S(1)}, u32[]{:S(2)}, u32[]{:S(2)}) collective-permute-start(bf16[192,768]{1,0:T(8,128)(2,1)S(1)} %fusion.12.refs_0_), channel_id=1, source_target_pairs={{8,0},{16,8},{24,16},{9,1},{17,9},{25,17},{10,2},{18,10},{26,18},{... | collective-permute-start | bytes 884744 | tf_op jit(solution)/shard_map/ppermute | solution.py:28
  11.1 41.7 %collective-permute-start = (bf16[192,768]{1,0:T(8,128)(2,1)S(1)}, bf16[192,768]{1,0:T(8,128)(2,1)S(1)}, u32[]{:S(2)}, u32[]{:S(2)}) collective-permute-start(bf16[192,768]{1,0:T(8,128)(2,1)S(1)} %fusion.12.refs_0_), channel_id=1, source_target_pairs={{0,8},{8,16},{16,24},{1,9},{9,17},{17,25},{2,10},{10,18},{18,26},{... | collective-permute-start | bytes 884744 | tf_op jit(solution)/shard_map/ppermute | solution.py:28
  17.3 13.6 %collective-permute-start.6 = (bf16[16,768]{1,0:T(8,128)(2,1)S(1)}, bf16[16,768]{1,0:T(8,128)(2,1)S(1)}, u32[]{:S(2)}, u32[]{:S(2)}) collective-permute-start(bf16[16,768]{1,0:T(8,128)(2,1)S(1)} %fusion.29), channel_id=1, source_target_pairs={{0,8},{8,0},{16,24},{24,16},{1,9},{9,1},{17,25},{25,17},{2,10},{10... | collective-permute-start | bytes 73736 | tf_op jit(solution)/shard_map/ppermute | solution.py:38
  52.9 12.4 %collective-permute-start.5 = (bf16[384,768]{1,0:T(8,128)(2,1)S(1)}, bf16[384,768]{1,0:T(8,128)(2,1)S(1)}, u32[]{:S(2)}, u32[]{:S(2)}) collective-permute-start(bf16[384,768]{1,0:T(8,128)(2,1)S(1)} %constant_dynamic-update-slice_fusion), channel_id=1, source_target_pairs={{2,0},{4,2},{6,4},{3,1},{5,3},{7,5},{10,8},{12,10},{14,12},{11,9},... | collective-permute-start | bytes 1769480 | tf_op jit(solution)/shard_map/ppermute | solution.py:28
  54.3 12.1 %collective-permute-start.4 = (bf16[384,768]{1,0:T(8,128)(2,1)S(1)}, bf16[384,768]{1,0:T(8,128)(2,1)S(1)}, u32[]{:S(2)}, u32[]{:S(2)}) collective-permute-start(bf16[384,768]{1,0:T(8,128)(2,1)S(1)} %constant_dynamic-update-slice_fusion), channel_id=1, source_target_pairs={{0,2},{2,4},{4,6},{1,3},{3,5},{5,7},{8,10},{10,12},{12,14},{9,11},... | collective-permute-start | bytes 1769480 | tf_op jit(solution)/shard_map/ppermute | solution.py:28
  106.8 29.2 %collective-permute-start.15 = (bf16[384,768]{1,0:T(8,128)(2,1)}, bf16[384,768]{1,0:T(8,128)(2,1)}, u32[]{:S(2)}, u32[]{:S(2)}) collective-permute-start(bf16[384,768]{1,0:T(8,128)(2,1)} %dynamic-slice_bitcast_fusion.1), channel_id=1, source_target_pairs={{0,8},{8,0},{16,24},{24,16},{1,9},{9,1},{17,25},{25,17},{2,10},{10... | collective-permute-start | bytes 1769480 | tf_op jit(solution)/shard_map/ppermute | solution.py:38
  112.6 94.9 %collective-permute-start.11 = (bf16[192,768]{1,0:T(8,128)(2,1)}, bf16[192,768]{1,0:T(8,128)(2,1)S(1)}, u32[]{:S(2)}, u32[]{:S(2)}) collective-permute-start(bf16[192,768]{1,0:T(8,128)(2,1)} %copy-done.11), channel_id=1, source_target_pairs={{0,2},{2,4},{4,6},{1,3},{3,5},{5,7},{8,10},{10,12},{12,14},{9,11},... | collective-permute-start | bytes 884744 | tf_op jit(solution)/shard_map/ppermute | solution.py:28
  117.1 29.0 %collective-permute-start.13 = (bf16[384,768]{1,0:T(8,128)(2,1)S(1)}, bf16[384,768]{1,0:T(8,128)(2,1)S(1)}, u32[]{:S(2)}, u32[]{:S(2)}) collective-permute-start(bf16[384,768]{1,0:T(8,128)(2,1)S(1)} %copy-done.8), channel_id=1, source_target_pairs={{0,2},{2,4},{4,6},{1,3},{3,5},{5,7},{8,10},{10,12},{12,14},{9,11},... | collective-permute-start | bytes 1769480 | tf_op jit(solution)/shard_map/ppermute | solution.py:28
  119.0 27.1 %collective-permute-start.14 = (bf16[384,768]{1,0:T(8,128)(2,1)S(1)}, bf16[384,768]{1,0:T(8,128)(2,1)S(1)}, u32[]{:S(2)}, u32[]{:S(2)}) collective-permute-start(bf16[384,768]{1,0:T(8,128)(2,1)S(1)} %copy-done.6), channel_id=1, source_target_pairs={{2,0},{4,2},{6,4},{3,1},{5,3},{7,5},{10,8},{12,10},{14,12},{11,9},... | collective-permute-start | bytes 1769480 | tf_op jit(solution)/shard_map/ppermute | solution.py:28
  121.4 22.3 %collective-permute-start.20 = (bf16[384,768]{1,0:T(8,128)(2,1)S(1)}, bf16[384,768]{1,0:T(8,128)(2,1)S(1)}, u32[]{:S(2)}, u32[]{:S(2)}) collective-permute-start(bf16[384,768]{1,0:T(8,128)(2,1)S(1)} %dynamic-slice_bitcast_fusion), channel_id=1, source_target_pairs={{0,16},{8,24},{16,0},{24,8},{1,17},{9,25},{17,1},{25,9},{2,18},{10... | collective-permute-start | bytes 1769480 | tf_op jit(solution)/shard_map/ppermute | solution.py:38
  137.3 9.6 %collective-permute-start.26 = (bf16[192,768]{1,0:T(8,128)(2,1)S(1)}, bf16[192,768]{1,0:T(8,128)(2,1)S(1)}, u32[]{:S(2)}, u32[]{:S(2)}) collective-permute-start(bf16[192,768]{1,0:T(8,128)(2,1)S(1)} %constant_dynamic-slice_fusion.13), channel_id=1, source_target_pairs={{0,16},{8,24},{16,0},{24,8},{1,17},{9,25},{17,1},{25,9},{2,18},{10... | collective-permute-start | bytes 884744 | tf_op jit(solution)/shard_map/ppermute | solution.py:38
  143.8 28.3 %collective-permute-start.16 = (bf16[384,768]{1,0:T(8,128)(2,1)S(1)}, bf16[384,768]{1,0:T(8,128)(2,1)S(1)}, u32[]{:S(2)}, u32[]{:S(2)}) collective-permute-start(bf16[384,768]{1,0:T(8,128)(2,1)S(1)} %constant_dynamic-slice_fusion.31), channel_id=1, source_target_pairs={{0,8},{8,0},{16,24},{24,16},{1,9},{9,1},{17,25},{25,17},{2,10},{10... | collective-permute-start | bytes 1769480 | tf_op jit(solution)/shard_map/ppermute | solution.py:38
  146.0 10.8 %collective-permute-start.27 = (bf16[192,768]{1,0:T(8,128)(2,1)S(1)}, bf16[192,768]{1,0:T(8,128)(2,1)S(1)}, u32[]{:S(2)}, u32[]{:S(2)}) collective-permute-start(bf16[192,768]{1,0:T(8,128)(2,1)S(1)} %constant_dynamic-slice_fusion.11), channel_id=1, source_target_pairs={{0,8},{8,0},{16,24},{24,16},{1,9},{9,1},{17,25},{25,17},{2,10},{10... | collective-permute-start | bytes 884744 | tf_op jit(solution)/shard_map/ppermute | solution.py:38
  160.2 8.6 %collective-permute-start.29 = (bf16[96,768]{1,0:T(8,128)(2,1)S(1)}, bf16[96,768]{1,0:T(8,128)(2,1)S(1)}, u32[]{:S(2)}, u32[]{:S(2)}) collective-permute-start(bf16[96,768]{1,0:T(8,128)(2,1)S(1)} %pad_maximum_fusion.6), channel_id=1, source_target_pairs={{0,4},{2,6},{4,0},{6,2},{1,5},{3,7},{5,1},{7,3},{8,12},{10,14},{12... | collective-permute-start | bytes 442376 | tf_op jit(solution)/shard_map/ppermute | solution.py:33
  160.4 10.4 %collective-permute-start.30 = (bf16[96,768]{1,0:T(8,128)(2,1)S(1)}, bf16[96,768]{1,0:T(8,128)(2,1)S(1)}, u32[]{:S(2)}, u32[]{:S(2)}) collective-permute-start(bf16[96,768]{1,0:T(8,128)(2,1)S(1)} %pad_maximum_fusion.7), channel_id=1, source_target_pairs={{0,6},{2,0},{4,2},{6,4},{1,7},{3,1},{5,3},{7,5},{8,14},{10,8},{12,... | collective-permute-start | bytes 442376 | tf_op jit(solution)/shard_map/ppermute | solution.py:33
  165.5 43.5 %collective-permute-start.12 = (bf16[192,768]{1,0:T(8,128)(2,1)S(1)}, bf16[192,768]{1,0:T(8,128)(2,1)S(1)}, u32[]{:S(2)}, u32[]{:S(2)}) collective-permute-start(bf16[192,768]{1,0:T(8,128)(2,1)S(1)} %copy-done.10), channel_id=1, source_target_pairs={{2,0},{4,2},{6,4},{3,1},{5,3},{7,5},{10,8},{12,10},{14,12},{11,9},... | collective-permute-start | bytes 884744 | tf_op jit(solution)/shard_map/ppermute | solution.py:28
  168.9 20.5 %collective-permute-start.21 = (bf16[512,768]{1,0:T(8,128)(2,1)S(1)}, bf16[512,768]{1,0:T(8,128)(2,1)S(1)}, u32[]{:S(2)}, u32[]{:S(2)}) collective-permute-start(bf16[512,768]{1,0:T(8,128)(2,1)S(1)} %pad_maximum_fusion), channel_id=1, source_target_pairs={{0,16},{8,24},{16,0},{24,8},{1,17},{9,25},{17,1},{25,9},{2,18},{10... | collective-permute-start | bytes 2359304 | tf_op jit(solution)/shard_map/ppermute | solution.py:38
  170.9 17.5 %collective-permute-start.33 = (bf16[96,768]{1,0:T(8,128)(2,1)S(1)}, bf16[96,768]{1,0:T(8,128)(2,1)S(1)}, u32[]{:S(2)}, u32[]{:S(2)}) collective-permute-start(bf16[96,768]{1,0:T(8,128)(2,1)S(1)} %get-tuple-element.34), channel_id=1, source_target_pairs={{0,2},{2,4},{4,6},{6,0},{1,3},{3,5},{5,7},{7,1},{8,10},{10,12},{12... | collective-permute-start | bytes 442376 | tf_op jit(solution)/shard_map/ppermute | solution.py:33
  178.2 9.0 %collective-permute-start.32 = (bf16[96,768]{1,0:T(8,128)(2,1)S(1)}, bf16[96,768]{1,0:T(8,128)(2,1)S(1)}, u32[]{:S(2)}, u32[]{:S(2)}) collective-permute-start(bf16[96,768]{1,0:T(8,128)(2,1)S(1)} %get-tuple-element.34), channel_id=1, source_target_pairs={{0,4},{2,6},{4,0},{6,2},{1,5},{3,7},{5,1},{7,3},{8,12},{10,14},{12... | collective-permute-start | bytes 442376 | tf_op jit(solution)/shard_map/ppermute | solution.py:33
  187.2 9.9 %collective-permute-start.17 = (bf16[192,768]{1,0:T(8,128)(2,1)S(1)}, bf16[192,768]{1,0:T(8,128)(2,1)S(1)}, u32[]{:S(2)}, u32[]{:S(2)}) collective-permute-start(bf16[192,768]{1,0:T(8,128)(2,1)S(1)} %constant_dynamic-slice_fusion.30), channel_id=1, source_target_pairs={{0,16},{8,24},{16,0},{24,8},{1,17},{9,25},{17,1},{25,9},{2,18},{10... | collective-permute-start | bytes 884744 | tf_op jit(solution)/shard_map/ppermute | solution.py:38
  188.5 10.5 %collective-permute-start.43 = (bf16[192,768]{1,0:T(8,128)(2,1)S(1)}, bf16[192,768]{1,0:T(8,128)(2,1)S(1)}, u32[]{:S(2)}, u32[]{:S(2)}) collective-permute-start(bf16[192,768]{1,0:T(8,128)(2,1)S(1)} %bitcast.111), channel_id=1, source_target_pairs={{0,8},{8,0},{16,24},{24,16},{1,9},{9,1},{17,25},{25,17},{2,10},{10... | collective-permute-start | bytes 884744 | tf_op jit(solution)/shard_map/ppermute | solution.py:38
  189.4 12.6 %collective-permute-start.34 = (bf16[192,768]{1,0:T(8,128)(2,1)S(1)}, bf16[192,768]{1,0:T(8,128)(2,1)S(1)}, u32[]{:S(2)}, u32[]{:S(2)}) collective-permute-start(bf16[192,768]{1,0:T(8,128)(2,1)S(1)} %bitcast.109), channel_id=1, source_target_pairs={{0,16},{8,24},{16,0},{24,8},{1,17},{9,25},{17,1},{25,9},{2,18},{10... | collective-permute-start | bytes 884744 | tf_op jit(solution)/shard_map/ppermute | solution.py:38
  199.1 10.0 %collective-permute-start.18 = (bf16[192,768]{1,0:T(8,128)(2,1)S(1)}, bf16[192,768]{1,0:T(8,128)(2,1)S(1)}, u32[]{:S(2)}, u32[]{:S(2)}) collective-permute-start(bf16[192,768]{1,0:T(8,128)(2,1)S(1)} %get-tuple-element.47), channel_id=1, source_target_pairs={{0,8},{8,16},{16,24},{1,9},{9,17},{17,25},{2,10},{10,18},{18,26},{... | collective-permute-start | bytes 884744 | tf_op jit(solution)/shard_map/ppermute | solution.py:28
  201.9 9.8 %collective-permute-start.19 = (bf16[192,768]{1,0:T(8,128)(2,1)S(1)}, bf16[192,768]{1,0:T(8,128)(2,1)S(1)}, u32[]{:S(2)}, u32[]{:S(2)}) collective-permute-start(bf16[192,768]{1,0:T(8,128)(2,1)S(1)} %get-tuple-element.48), channel_id=1, source_target_pairs={{8,0},{16,8},{24,16},{9,1},{17,9},{25,17},{10,2},{18,10},{26,18},{... | collective-permute-start | bytes 884744 | tf_op jit(solution)/shard_map/ppermute | solution.py:28
  204.8 37.1 %collective-permute-start.35 = (bf16[384,768]{1,0:T(8,128)(2,1)S(1)}, bf16[384,768]{1,0:T(8,128)(2,1)S(1)}, u32[]{:S(2)}, u32[]{:S(2)}) collective-permute-start(bf16[384,768]{1,0:T(8,128)(2,1)S(1)} %maximum_select_fusion.4), channel_id=1, source_target_pairs={{0,8},{8,0},{16,24},{24,16},{1,9},{9,1},{17,25},{25,17},{2,10},{10... | collective-permute-start | bytes 1769480 | tf_op jit(solution)/shard_map/ppermute | solution.py:38
  207.6 34.9 %collective-permute-start.44 = (bf16[384,768]{1,0:T(8,128)(2,1)S(1)}, bf16[384,768]{1,0:T(8,128)(2,1)S(1)}, u32[]{:S(2)}, u32[]{:S(2)}) collective-permute-start(bf16[384,768]{1,0:T(8,128)(2,1)S(1)} %maximum_select_fusion.7), channel_id=1, source_target_pairs={{0,16},{8,24},{16,0},{24,8},{1,17},{9,25},{17,1},{25,9},{2,18},{10... | collective-permute-start | bytes 1769480 | tf_op jit(solution)/shard_map/ppermute | solution.py:38
  209.1 10.1 %collective-permute-start.24 = (bf16[112,768]{1,0:T(8,128)(2,1)S(1)}, bf16[112,768]{1,0:T(8,128)(2,1)S(1)}, u32[]{:S(2)}, u32[]{:S(2)}) collective-permute-start(bf16[112,768]{1,0:T(8,128)(2,1)S(1)} %pad_maximum_fusion.3), channel_id=1, source_target_pairs={{0,4},{2,6},{4,0},{6,2},{1,5},{3,7},{5,1},{7,3},{8,12},{10,14},{12... | collective-permute-start | bytes 516104 | tf_op jit(solution)/shard_map/ppermute | solution.py:33
  232.3 8.7 %collective-permute-start.41 = (bf16[192,768]{1,0:T(8,128)(2,1)S(1)}, bf16[192,768]{1,0:T(8,128)(2,1)S(1)}, u32[]{:S(2)}, u32[]{:S(2)}) collective-permute-start(bf16[192,768]{1,0:T(8,128)(2,1)S(1)} %bitcast.113), channel_id=1, source_target_pairs={{0,8},{8,0},{16,24},{24,16},{1,9},{9,1},{17,25},{25,17},{2,10},{10... | collective-permute-start | bytes 884744 | tf_op jit(solution)/shard_map/ppermute | solution.py:38
  238.5 10.3 %collective-permute-start.40 = (bf16[384,768]{1,0:T(8,128)(2,1)S(1)}, bf16[384,768]{1,0:T(8,128)(2,1)S(1)}, u32[]{:S(2)}, u32[]{:S(2)}) collective-permute-start(bf16[384,768]{1,0:T(8,128)(2,1)S(1)} %maximum_select_fusion.5), channel_id=1, source_target_pairs={{0,8},{8,0},{16,24},{24,16},{1,9},{9,1},{17,25},{25,17},{2,10},{10... | collective-permute-start | bytes 1769480 | tf_op jit(solution)/shard_map/ppermute | solution.py:38
  241.2 9.9 %collective-permute-start.42 = (bf16[384,768]{1,0:T(8,128)(2,1)S(1)}, bf16[384,768]{1,0:T(8,128)(2,1)S(1)}, u32[]{:S(2)}, u32[]{:S(2)}) collective-permute-start(bf16[384,768]{1,0:T(8,128)(2,1)S(1)} %maximum_select_fusion.6), channel_id=1, source_target_pairs={{0,16},{8,24},{16,0},{24,8},{1,17},{9,25},{17,1},{25,9},{2,18},{10... | collective-permute-start | bytes 1769480 | tf_op jit(solution)/shard_map/ppermute | solution.py:38
  (39 other events, 259.3 us)
where the time goes:
time: 259 us; the launch traced here: 258 us
  starting transfers between devices  104 us (40%)
  waiting for transfers between devices  81.3 us (31%)
  Pallas kernels  32.6 us (13%)
  local copies, waits for them, and re-layouts  16.6 us (6%)
  other arithmetic  16.5 us (6%)
  matrix products  5.15 us (2%)
    ppermute x18, starting transfers between devices, swapped(): return lax.ppermute(array, axis, [(i, i ^ 1 << bit) for i in range(peers)])  42.3 us
    ppermute x18, waiting for transfers between devices, swapped(): return lax.ppermute(array, axis, [(i, i ^ 1 << bit) for i in range(peers)])  39.9 us
    ppermute x15, waiting for transfers between devices, rotated(): lax.ppermute(array, axis, [(i, (i + by) % peers) for i in range(peers)])  34.1 us
    pallas_call x1, Pallas kernels, layer(): pl.pallas_call(functools.partial(layer_kernel, segments, len(sources)), i...  32.6 us
    ppermute x12, starting transfers between devices, shifted(): return lax.ppermute(array, axis, pairs)  31.1 us
    ppermute x15, starting transfers between devices, rotated(): lax.ppermute(array, axis, [(i, (i + by) % peers) for i in range(peers)])  30.2 us
    ppermute x12, waiting for transfers between devices, shifted(): return lax.ppermute(array, axis, pairs)  7.28 us
    unnamed x71, local copies, waits for them, and re-layouts  7.06 us
  transfers between devices with their start and end apart: 45, of which 24 were waited for; matrix products, arithmetic and copies ran while one was open for 8% of the time, Pallas kernels for 0%

commit v1 on v0

--- a/solution.py
+++ b/solution.py
@@ -56,9 +56,10 @@
 def layer_kernel(segments, n_in, meta, tokens, query, grad, masked, weights, *refs):
     sources = refs[:n_in]
     outs = refs[n_in:]
-    updated_ref, dw_ref = outs[:2]
-    targets = outs[2 : 2 + n_in]
-    (hc, hct, bias, k_s, v_s, e_s, acc_s, o_s, dq_s, dw_s) = outs[2 + n_in :]
+    updated_ref = outs[0]
+    dw_refs = outs[1:5]
+    targets = outs[5 : 5 + n_in]
+    (hc, hct, bias, k_s, v_s, e_s, p_s, acc_s, o_s, dq_s, dw_s) = outs[5 + n_in :]
     own_ref = sources[0]
     n_seg = len(segments)
     rows = own_ref.shape[0]
@@ -147,6 +148,7 @@
             at = chunk_at(c)
             e = jnp.exp(e_s[i % 2, at, :] - top)
             e_s[i % 2, at, :] = e
+            p_s[at, :] = mm(v_s[at, cols], g2t)
             acc_s[...] += mm(v_s[at, cols], e.astype(bf16), ((0,), (0,)))
             return sums + jnp.sum(e.reshape(CHUNK // 8, 8, lanes), axis=0)
 
@@ -165,7 +167,7 @@
             if more:
                 largest = score(i + 1, c, q2t, largest)
             probs = e_s[i % 2, at, :] * inverse
-            dscore = (probs * (mm(v_s[at, cols], g2t) - delta)).astype(bf16)
+            dscore = (probs * (p_s[at, :] - delta)).astype(bf16)
             acc_s[...] += mm(k_s[at, cols], dscore, ((0,), (0,)))
             k_s[at, cols] = mm(dscore, q2).astype(bf16)
             v_s[at, cols] = mm(probs.astype(bf16), g2).astype(bf16)
@@ -183,8 +185,8 @@
         cut = slice(n, n + 256)
         moved = jnp.where(live, mm(attended, weights[3, :, cut]), 0.0)
         updated_ref[:, cut] = (tokens[:, cut].astype(f32) + moved).astype(bf16)
-        dw_ref[0, :, cut] = mm(own_t, dquery[:, cut]).astype(bf16)
-        dw_ref[3, :, cut] = mm(attended_t, masked[:, cut]).astype(bf16)
+        dw_refs[0][:, cut] = mm(own_t, dquery[:, cut]).astype(bf16)
+        dw_refs[3][:, cut] = mm(attended_t, masked[:, cut]).astype(bf16)
         targets[0][:, cut] = mm(dquery, weights[0, cut, :], ((1,), (1,)))
     for source, into in ((k_s, 1), (v_s, 2)):
 
@@ -196,7 +198,7 @@
 
         dw_s[...] = jnp.zeros_like(dw_s)
         lax.fori_loop(0, blocks, outer, 0)
-        dw_ref[into] = dw_s[...].astype(bf16)
+        dw_refs[into][...] = dw_s[...].astype(bf16)
 
     def returned(c, carry):
         at = block_at(c)
@@ -235,7 +237,7 @@
     vmem = pl.BlockSpec(memory_space=pltpu.VMEM)
     out_shape = [
         jax.ShapeDtypeStruct((rows, width), bf16),
-        jax.ShapeDtypeStruct((4, width, width), bf16),
+        *[jax.ShapeDtypeStruct((width, width), bf16)] * 4,
         jax.ShapeDtypeStruct((rows, width), f32),
     ] + [jax.ShapeDtypeStruct(a.shape, bf16) for a in sources[1:]]
     scratch = [
@@ -245,12 +247,13 @@
         pltpu.VMEM((room, width), bf16),
         pltpu.VMEM((room, width), bf16),
         pltpu.VMEM((2, room, 2 * rows), f32),
+        pltpu.VMEM((room, 2 * rows), f32),
         pltpu.VMEM((128, 2 * rows), f32),
         pltpu.VMEM((rows, width), bf16),
         pltpu.VMEM((rows, width), bf16),
         pltpu.VMEM((width, width), f32),
     ]
-    held = room * (3 * width * 2 + width * 2 + 512 + 16 * rows) + 6 * width * width * 4
+    held = room * (3 * width * 2 + width * 2 + 512 + 24 * rows) + 6 * width * width * 4
     grant = held + 4 * most * width + 6 * 2**20
     return pl.pallas_call(
         functools.partial(layer_kernel, segments, len(sources)),
@@ -347,26 +350,20 @@
 
     bits = split_bits(n_ty)
     back_bits = bits[::-1]
-    gathered = summary_hidden
-    for b in bits:
-        gathered = unfold(gathered, "ty", b, row)
     up = shifted(hidden, "ty", 1)
     down = shifted(hidden, "ty", -1)
     left = shifted(hidden, "tx", 1)
     right = shifted(hidden, "tx", -1)
-    columns = [gathered]
+    columns = [summary_hidden]
     for k in range(1, n_tx):
-        columns.append(rotated(gathered, "tx", k))
+        columns.append(rotated(summary_hidden, "tx", k))
     both = jnp.concatenate([up, down], axis=0)
     left_two = shifted(both, "tx", 1)
     right_two = shifted(both, "tx", -1)
     each = summary.shape[0]
-    every_summary = (
-        in_order(columns, col)
-        .reshape(n_tx, n_ty, each, width)
-        .transpose(1, 0, 2, 3)
-        .reshape(n_ty * n_tx * each, width)
-    )
+    every_summary = in_order(columns, col).reshape(n_tx * each, width)
+    for b in bits:
+        every_summary = unfold(every_summary, "ty", b, row)
 
     live = jnp.arange(tile, dtype=jnp.int32)[:, None] < lax.dynamic_slice(
         counts, (row, col), (1, 1)
@@ -397,8 +394,8 @@
     ) + tuple((7, SBLK * b) for b in range(summary_pattern.shape[2]))
     sources = [hidden, up, down, left, right, left_two, right_two, every_summary]
     results = layer(meta, segments, rows, query, grad, masked, sources, projections)
-    updated, dw = results[:2]
-    d_own, d_up, d_down, d_left, d_right, d_left_two, d_right_two, d_summary = results[2:]
+    updated, dw = results[0], results[1:5]
+    d_own, d_up, d_down, d_left, d_right, d_left_two, d_right_two, d_summary = results[5:]
 
     def halves(left_list, right_list, level):
         return (
@@ -424,7 +421,7 @@
         + far_right.astype(f32)
         + far_left.astype(f32)
     ).astype(bf16)
-    pair_sum = after(pair_sum, *two[0])
+    pair_sum = after(pair_sum, *two[0], *two[1])
     from_above = shifted(pair_sum[tile:], "ty", 1)
     from_below = shifted(pair_sum[:tile], "ty", -1)
     hidden_grad = (
@@ -434,13 +431,18 @@
         + from_above.astype(f32)
         + from_below.astype(f32)
     )
-    two = fold_line(two[0] + two[1], "tx", col)
+    folded = two[0] + two[1]
+    two = fold_line(folded, "tx", col)
     summary_hidden_grad = two[-each:]
     two = two[:-each].astype(bf16)
 
-    def spread(block):
-        pieces = [block] + [rotated(block, "tx", k) for k in range(1, n_tx)]
+    def spread(block, *wait):
+        pieces = [block]
+        for k in range(1, n_tx):
+            pieces.append(rotated(block, "tx", k))
         stacked = in_order(pieces, col)
+        if wait:
+            stacked = after(stacked, *wait)
         size = block.shape[0] // 2
         a = stacked[:, :size].reshape(n_tx * size, width)
         b = stacked[:, size:].reshape(n_tx * size, width)
@@ -449,7 +451,7 @@
             b = unfold(b, "ty", back_bits[level], row)
         return a, b
 
-    g_query, g_out = spread(one)
+    g_query, g_out = spread(one, *folded)
     g_key, g_value = spread(two)
     grad_proj = jnp.stack([g_query, g_key, g_value, g_out]).astype(f32)
     grad_gain = jnp.sum(grad_proj[:3] * projections[:3].astype(f32), axis=(0, 2)) / norm_gain

time: 259 us -> 250 us (0.965)
  waiting for transfers between devices: 81.3 us -> 74.3 us
  starting transfers between devices: 104 us -> 99.7 us
  local copies, waits for them, and re-layouts: 16.6 us -> 20 us
  Pallas kernels: 32.6 us -> 29.9 us
    ppermute x12, waiting for transfers between devices: 7.28 us -> 23 us  [shifted(): return lax.ppermute(array, axis, pairs)]
    ppermute x18, waiting for transfers between devices: 39.9 us -> 25.5 us  [swapped(): return lax.ppermute(array, axis, [(i, i ^ 1 << bit) for i in range(peers)])]
    ppermute x18, starting transfers between devices: 42.3 us -> 28.6 us  [swapped(): return lax.ppermute(array, axis, [(i, i ^ 1 << bit) for i in range(peers)])]
    ppermute x12, starting transfers between devices: 31.1 us -> 40.8 us  [shifted(): return lax.ppermute(array, axis, pairs)]
    ppermute x15, waiting for transfers between devices: 34.1 us -> 25.8 us  [rotated(): lax.ppermute(array, axis, [(i, (i + by) % peers) for i in range(peers)])]
    unnamed x71 -> x72, local copies, waits for them, and re-layouts: 7.06 us -> 12.6 us
    slice x1 -> x0, local copies, waits for them, and re-layouts: 4.85 us -> none  [local(): one = ([dw[0]], [dw[3]])]
    pallas_call x1, Pallas kernels: 32.6 us -> 29.9 us  [layer(): pl.pallas_call(functools.partial(layer_kernel, segments, len(sources)), i...]
  transfers between devices with their start and end apart: 45 -> 45, of which waited for: 24 -> 19; matrix products, arithmetic and copies ran while one was open for 8% -> 10% of each run, Pallas kernels for 0% -> 0%
where the time goes in v1:
time: 250 us; the launch traced here: 249 us
  starting transfers between devices  99.7 us (40%)
  waiting for transfers between devices  74.3 us (30%)
  Pallas kernels  29.9 us (12%)
  local copies, waits for them, and re-layouts  20 us (8%)
  other arithmetic  17.8 us (7%)
  matrix products  5.15 us (2%)
    ppermute x12, starting transfers between devices, shifted(): return lax.ppermute(array, axis, pairs)  40.8 us
    ppermute x15, starting transfers between devices, rotated(): lax.ppermute(array, axis, [(i, (i + by) % peers) for i in range(peers)])  30.3 us
    pallas_call x1, Pallas kernels, layer(): pl.pallas_call(functools.partial(layer_kernel, segments, len(sources)), i...  29.9 us
    ppermute x18, starting transfers between devices, swapped(): return lax.ppermute(array, axis, [(i, i ^ 1 << bit) for i in range(peers)])  28.6 us
    ppermute x15, waiting for transfers between devices, rotated(): lax.ppermute(array, axis, [(i, (i + by) % peers) for i in range(peers)])  25.8 us
    ppermute x18, waiting for transfers between devices, swapped(): return lax.ppermute(array, axis, [(i, i ^ 1 << bit) for i in range(peers)])  25.5 us
    ppermute x12, waiting for transfers between devices, shifted(): return lax.ppermute(array, axis, pairs)  23 us
    unnamed x72, local copies, waits for them, and re-layouts  12.6 us
  transfers between devices with their start and end apart: 45, of which 19 were waited for; matrix products, arithmetic and copies ran while one was open for 10% of the time, Pallas kernels for 0%

profile of v1, /device:TPU:0, one launch (start us, length us, event | category | flops | bytes accessed | tf_op | source)
XLA Modules:
  0.0 249.0 jit_solution(16475044965667363141)
XLA Ops:
  2.3 3.1 %collective-permute-start.8 = (bf16[16,768]{1,0:T(8,128)(2,1)S(1)}, bf16[16,768]{1,0:T(8,128)(2,1)S(1)}, u32[]{:S(2)}, u32[]{:S(2)}) collective-permute-start(bf16[16,768]{1,0:T(8,128)(2,1)S(1)} %get-tuple-element.46), channel_id=1, source_target_pairs={{0,2},{2,4},{4,6},{6,0},{1,3},{3,5},{5,7},{7,1},{8,10},{10,12},{12... | collective-permute-start | bytes 73736 | tf_op jit(solution)/shard_map/ppermute | solution.py:33
  5.4 2.6 %collective-permute-start.7 = (bf16[16,768]{1,0:T(8,128)(2,1)S(1)}, bf16[16,768]{1,0:T(8,128)(2,1)S(1)}, u32[]{:S(2)}, u32[]{:S(2)}) collective-permute-start(bf16[16,768]{1,0:T(8,128)(2,1)S(1)} %get-tuple-element.46), channel_id=1, source_target_pairs={{0,4},{2,6},{4,0},{6,2},{1,5},{3,7},{5,1},{7,3},{8,12},{10,14},{12... | collective-permute-start | bytes 73736 | tf_op jit(solution)/shard_map/ppermute | solution.py:33
  12.9 4.6 %collective-permute-start.2 = (bf16[192,768]{1,0:T(8,128)(2,1)S(1)}, bf16[192,768]{1,0:T(8,128)(2,1)S(1)}, u32[]{:S(2)}, u32[]{:S(2)}) collective-permute-start(bf16[192,768]{1,0:T(8,128)(2,1)S(1)} %fusion.10.refs_0_), channel_id=1, source_target_pairs={{0,2},{2,4},{4,6},{1,3},{3,5},{5,7},{8,10},{10,12},{12,14},{9,11},... | collective-permute-start | bytes 884744 | tf_op jit(solution)/shard_map/ppermute | solution.py:28
  19.4 2.6 %fusion.5.query = bf16[192,768]{1,0:T(8,128)(2,1)} fusion(bf16[4,768,768]{2,1,0:T(8,128)(2,1)} %weights.1, bf16[1,1,192,768]{3,2,1,0:T(8,128)(2,1)} %param.8, f32[768]{0:T(1024)} %param.13, f32[192]{0:T(256)S(1)} %get-tuple-element.76), kind=kOutput, calls=%fused_computation.18 | convolution fusion | flops 227377152 | bytes 1774336 | tf_op jit(solution)/shard_map/dot_general | solution.py:53
  22.1 2.6 %convolution_convert_fusion.grad = bf16[192,768]{1,0:T(8,128)(2,1)} fusion(bf16[4,768,768]{2,1,0:T(8,128)(2,1)} %weights.1, bf16[1,1,192,768]{3,2,1,0:T(8,128)(2,1)S(1)} %copy-done.14, pred[192]{0:T(512)(128)(4,1)S(1)} %iota_compare_fusion), kind=kOutput, calls=%fused_computation.3 | convolution fusion | flops 226787328 | bytes 1769664 | tf_op jit(solution)/shard_map/dot_general | solution.py:53
  27.4 4.6 %collective-permute-start = (bf16[192,768]{1,0:T(8,128)(2,1)S(1)}, bf16[192,768]{1,0:T(8,128)(2,1)S(1)}, u32[]{:S(2)}, u32[]{:S(2)}) collective-permute-start(bf16[192,768]{1,0:T(8,128)(2,1)S(1)} %fusion.10.refs_0_), channel_id=1, source_target_pairs={{0,8},{8,16},{16,24},{1,9},{9,17},{17,25},{2,10},{10,18},{18,26},{... | collective-permute-start | bytes 884744 | tf_op jit(solution)/shard_map/ppermute | solution.py:28
  32.1 4.5 %collective-permute-done.refs_1_ = bf16[192,768]{1,0:T(8,128)(2,1)S(1)} collective-permute-done((bf16[192,768]{1,0:T(8,128)(2,1)S(1)}, bf16[192,768]{1,0:T(8,128)(2,1)S(1)}, u32[]{:S(2)}, u32[]{:S(2)}) %collective-permute-start) | collective-permute-done | bytes 294944 | tf_op jit(solution)/shard_map/ppermute | solution.py:28
  39.7 5.4 %collective-permute-start.4 = (bf16[384,768]{1,0:T(8,128)(2,1)}, bf16[384,768]{1,0:T(8,128)(2,1)}, u32[]{:S(2)}, u32[]{:S(2)}) collective-permute-start(bf16[384,768]{1,0:T(8,128)(2,1)} %constant_dynamic-update-slice_fusion), channel_id=1, source_target_pairs={{0,2},{2,4},{4,6},{1,3},{3,5},{5,7},{8,10},{10,12},{12,14},{9,11},... | collective-permute-start | bytes 1769480 | tf_op jit(solution)/shard_map/ppermute | solution.py:28
  45.1 4.3 %collective-permute-start.9 = (bf16[64,768]{1,0:T(8,128)(2,1)S(1)}, bf16[64,768]{1,0:T(8,128)(2,1)S(1)}, u32[]{:S(2)}, u32[]{:S(2)}) collective-permute-start(bf16[64,768]{1,0:T(8,128)(2,1)S(1)} %bitcast.103), channel_id=1, source_target_pairs={{0,8},{8,0},{16,24},{24,16},{1,9},{9,1},{17,25},{25,17},{2,10},{10... | collective-permute-start | bytes 294920 | tf_op jit(solution)/shard_map/ppermute | solution.py:38
  52.0 4.0 %collective-permute-start.10 = (bf16[128,768]{1,0:T(8,128)(2,1)S(1)}, bf16[128,768]{1,0:T(8,128)(2,1)S(1)}, u32[]{:S(2)}, u32[]{:S(2)}) collective-permute-start(bf16[128,768]{1,0:T(8,128)(2,1)S(1)} %maximum_select_fusion.9), channel_id=1, source_target_pairs={{0,16},{8,24},{16,0},{24,8},{1,17},{9,25},{17,1},{25,9},{2,18},{10... | collective-permute-start | bytes 589832 | tf_op jit(solution)/shard_map/ppermute | solution.py:38
  56.8 2.9 %collective-permute-done.10 = bf16[128,768]{1,0:T(8,128)(2,1)S(1)} collective-permute-done((bf16[128,768]{1,0:T(8,128)(2,1)S(1)}, bf16[128,768]{1,0:T(8,128)(2,1)S(1)}, u32[]{:S(2)}, u32[]{:S(2)}) %collective-permute-start.10) | collective-permute-done | bytes 196640 | tf_op jit(solution)/shard_map/ppermute | solution.py:38
  64.2 29.9 %layer.1 = (bf16[192,768]{1,0:T(8,128)(2,1)}, bf16[768,768]{1,0:T(8,128)(2,1)}, bf16[768,768]{1,0:T(8,128)(2,1)}, bf16[768,768]{1,0:T(8,128)(2,1)}, bf16[768,768...) custom-call(s32[2,12]{1,0:T(2,128)S(1)} %pad_add_fusion.meta, ...), custom_call_target="tpu_custom_call" | custom-call | tf_op jit(solution)/shard_map/layer/pallas_call | solution.py:258
  103.3 3.5 %collective-permute-start.15 = (bf16[384,768]{1,0:T(8,128)(2,1)}, bf16[384,768]{1,0:T(8,128)(2,1)}, u32[]{:S(2)}, u32[]{:S(2)}) collective-permute-start(bf16[384,768]{1,0:T(8,128)(2,1)} %constant_dynamic-slice_fusion.32), channel_id=1, source_target_pairs={{0,8},{8,0},{16,24},{24,16},{1,9},{9,1},{17,25},{25,17},{2,10},{10... | collective-permute-start | bytes 1769480 | tf_op jit(solution)/shard_map/ppermute | solution.py:38
  106.8 14.9 %collective-permute-start.11 = (bf16[192,768]{1,0:T(8,128)(2,1)S(1)}, bf16[192,768]{1,0:T(8,128)(2,1)S(1)}, u32[]{:S(2)}, u32[]{:S(2)}) collective-permute-start(bf16[192,768]{1,0:T(8,128)(2,1)S(1)} %copy-done.12), channel_id=1, source_target_pairs={{0,2},{2,4},{4,6},{1,3},{3,5},{5,7},{8,10},{10,12},{12,14},{9,11},... | collective-permute-start | bytes 884744 | tf_op jit(solution)/shard_map/ppermute | solution.py:28
  130.0 8.6 %collective-permute-done.13 = bf16[384,768]{1,0:T(8,128)(2,1)S(1)} collective-permute-done((bf16[384,768]{1,0:T(8,128)(2,1)S(1)}, bf16[384,768]{1,0:T(8,128)(2,1)S(1)}, u32[]{:S(2)}, u32[]{:S(2)}) %collective-permute-start.13) | collective-permute-done | bytes 589856 | tf_op jit(solution)/shard_map/ppermute | solution.py:28
  139.7 2.9 %collective-permute-done.14 = bf16[384,768]{1,0:T(8,128)(2,1)S(1)} collective-permute-done((bf16[384,768]{1,0:T(8,128)(2,1)S(1)}, bf16[384,768]{1,0:T(8,128)(2,1)S(1)}, u32[]{:S(2)}, u32[]{:S(2)}) %collective-permute-start.14) | collective-permute-done | bytes 589856 | tf_op jit(solution)/shard_map/ppermute | solution.py:28
  148.0 3.7 %collective-permute-done.28 = bf16[96,768]{1,0:T(8,128)(2,1)S(1)} collective-permute-done((bf16[96,768]{1,0:T(8,128)(2,1)S(1)}, bf16[96,768]{1,0:T(8,128)(2,1)S(1)}, u32[]{:S(2)}, u32[]{:S(2)}) %collective-permute-start.28) | collective-permute-done | bytes 147488 | tf_op jit(solution)/shard_map/ppermute | solution.py:33
  157.0 2.5 %collective-permute-start.31 = (bf16[96,768]{1,0:T(8,128)(2,1)S(1)}, bf16[96,768]{1,0:T(8,128)(2,1)S(1)}, u32[]{:S(2)}, u32[]{:S(2)}) collective-permute-start(bf16[96,768]{1,0:T(8,128)(2,1)S(1)} %get-tuple-element.42), channel_id=1, source_target_pairs={{0,6},{2,0},{4,2},{6,4},{1,7},{3,1},{5,3},{7,5},{8,14},{10,8},{12,... | collective-permute-start | bytes 442376 | tf_op jit(solution)/shard_map/ppermute | solution.py:33
  159.7 3.2 %collective-permute-done.31 = bf16[96,768]{1,0:T(8,128)(2,1)S(1)} collective-permute-done((bf16[96,768]{1,0:T(8,128)(2,1)S(1)}, bf16[96,768]{1,0:T(8,128)(2,1)S(1)}, u32[]{:S(2)}, u32[]{:S(2)}) %collective-permute-start.31) | collective-permute-done | bytes 147488 | tf_op jit(solution)/shard_map/ppermute | solution.py:33
  162.9 6.7 %collective-permute-start.32 = (bf16[96,768]{1,0:T(8,128)(2,1)S(1)}, bf16[96,768]{1,0:T(8,128)(2,1)S(1)}, u32[]{:S(2)}, u32[]{:S(2)}) collective-permute-start(bf16[96,768]{1,0:T(8,128)(2,1)S(1)} %get-tuple-element.42), channel_id=1, source_target_pairs={{0,4},{2,6},{4,0},{6,2},{1,5},{3,7},{5,1},{7,3},{8,12},{10,14},{12... | collective-permute-start | bytes 442376 | tf_op jit(solution)/shard_map/ppermute | solution.py:33
  169.7 5.9 %collective-permute-done.32 = bf16[96,768]{1,0:T(8,128)(2,1)S(1)} collective-permute-done((bf16[96,768]{1,0:T(8,128)(2,1)S(1)}, bf16[96,768]{1,0:T(8,128)(2,1)S(1)}, u32[]{:S(2)}, u32[]{:S(2)}) %collective-permute-start.32) | collective-permute-done | bytes 147488 | tf_op jit(solution)/shard_map/ppermute | solution.py:33
  176.3 7.8 %collective-permute-done.17 = bf16[192,768]{1,0:T(8,128)(2,1)S(1)} collective-permute-done((bf16[192,768]{1,0:T(8,128)(2,1)S(1)}, bf16[192,768]{1,0:T(8,128)(2,1)S(1)}, u32[]{:S(2)}, u32[]{:S(2)}) %collective-permute-start.17) | collective-permute-done | bytes 294944 | tf_op jit(solution)/shard_map/ppermute | solution.py:38
  184.2 2.8 %collective-permute-done.20 = bf16[256,768]{1,0:T(8,128)(2,1)S(1)} collective-permute-done((bf16[256,768]{1,0:T(8,128)(2,1)S(1)}, bf16[256,768]{1,0:T(8,128)(2,1)S(1)}, u32[]{:S(2)}, u32[]{:S(2)}) %collective-permute-start.20) | collective-permute-done | bytes 393248 | tf_op jit(solution)/shard_map/ppermute | solution.py:38
  188.4 3.5 %collective-permute-start.24 = (bf16[112,768]{1,0:T(8,128)(2,1)S(1)}, bf16[112,768]{1,0:T(8,128)(2,1)S(1)}, u32[]{:S(2)}, u32[]{:S(2)}) collective-permute-start(bf16[112,768]{1,0:T(8,128)(2,1)S(1)} %pad_maximum_fusion.3), channel_id=1, source_target_pairs={{0,4},{2,6},{4,0},{6,2},{1,5},{3,7},{5,1},{7,3},{8,12},{10,14},{12... | collective-permute-start | bytes 516104 | tf_op jit(solution)/shard_map/ppermute | solution.py:33
  192.0 2.7 %collective-permute-done.23 = bf16[112,768]{1,0:T(8,128)(2,1)S(1)} collective-permute-done((bf16[112,768]{1,0:T(8,128)(2,1)S(1)}, bf16[112,768]{1,0:T(8,128)(2,1)S(1)}, u32[]{:S(2)}, u32[]{:S(2)}) %collective-permute-start.23) | collective-permute-done | bytes 172064 | tf_op jit(solution)/shard_map/ppermute | solution.py:33
  199.7 3.6 %collective-permute-start.43 = (bf16[192,768]{1,0:T(8,128)(2,1)S(1)}, bf16[192,768]{1,0:T(8,128)(2,1)S(1)}, u32[]{:S(2)}, u32[]{:S(2)}) collective-permute-start(bf16[192,768]{1,0:T(8,128)(2,1)S(1)} %bitcast.91), channel_id=1, source_target_pairs={{0,8},{8,0},{16,24},{24,16},{1,9},{9,1},{17,25},{25,17},{2,10},{10... | collective-permute-start | bytes 884744 | tf_op jit(solution)/shard_map/ppermute | solution.py:38
  205.8 2.6 %collective-permute-start.36 = (bf16[96,768]{1,0:T(8,128)(2,1)S(1)}, bf16[96,768]{1,0:T(8,128)(2,1)S(1)}, u32[]{:S(2)}, u32[]{:S(2)}) collective-permute-start(bf16[96,768]{1,0:T(8,128)(2,1)S(1)} %get-tuple-element.40), channel_id=1, source_target_pairs={{0,6},{2,0},{4,2},{6,4},{1,7},{3,1},{5,3},{7,5},{8,14},{10,8},{12,... | collective-permute-start | bytes 442376 | tf_op jit(solution)/shard_map/ppermute | solution.py:33
  208.4 6.7 %collective-permute-done.22 = bf16[192,768]{1,0:T(8,128)(2,1)S(1)} collective-permute-done((bf16[192,768]{1,0:T(8,128)(2,1)S(1)}, bf16[192,768]{1,0:T(8,128)(2,1)S(1)}, u32[]{:S(2)}, u32[]{:S(2)}) %collective-permute-start.22) | collective-permute-done | bytes 294944 | tf_op jit(solution)/shard_map/ppermute | solution.py:28
  215.5 6.5 %collective-permute-done.38 = bf16[96,768]{1,0:T(8,128)(2,1)S(1)} collective-permute-done((bf16[96,768]{1,0:T(8,128)(2,1)S(1)}, bf16[96,768]{1,0:T(8,128)(2,1)S(1)}, u32[]{:S(2)}, u32[]{:S(2)}) %collective-permute-start.38) | collective-permute-done | bytes 147488 | tf_op jit(solution)/shard_map/ppermute | solution.py:33
  232.2 3.2 %collective-permute-done.35 = bf16[384,768]{1,0:T(8,128)(2,1)S(1)} collective-permute-done((bf16[384,768]{1,0:T(8,128)(2,1)S(1)}, bf16[384,768]{1,0:T(8,128)(2,1)S(1)}, u32[]{:S(2)}, u32[]{:S(2)}) %collective-permute-start.35) | collective-permute-done | bytes 589856 | tf_op jit(solution)/shard_map/ppermute | solution.py:38
  236.4 5.4 %collective-permute-done.40 = bf16[384,768]{1,0:T(8,128)(2,1)S(1)} collective-permute-done((bf16[384,768]{1,0:T(8,128)(2,1)S(1)}, bf16[384,768]{1,0:T(8,128)(2,1)S(1)}, u32[]{:S(2)}, u32[]{:S(2)}) %collective-permute-start.40) | collective-permute-done | bytes 589856 | tf_op jit(solution)/shard_map/ppermute | solution.py:38
  245.4 3.0 %copy-done.13 = f32[4,768,768]{2,1,0:T(8,128)} copy-done((f32[4,768,768]{2,1,0:T(8,128)}, f32[4,768,768]{2,1,0:T(8,128)S(1)}, u32[]{:S(2)}) %copy-start.13) | copy-done | bytes 9437208
  (215 shorter events, 76.1 us)
Async XLA Ops:
  2.3 29.7 %collective-permute-start.8 = (bf16[16,768]{1,0:T(8,128)(2,1)S(1)}, bf16[16,768]{1,0:T(8,128)(2,1)S(1)}, u32[]{:S(2)}, u32[]{:S(2)}) collective-permute-start(bf16[16,768]{1,0:T(8,128)(2,1)S(1)} %get-tuple-element.46), channel_id=1, source_target_pairs={{0,2},{2,4},{4,6},{6,0},{1,3},{3,5},{5,7},{7,1},{8,10},{10,12},{12... | collective-permute-start | bytes 73736 | tf_op jit(solution)/shard_map/ppermute | solution.py:33
  5.4 22.0 %collective-permute-start.7 = (bf16[16,768]{1,0:T(8,128)(2,1)S(1)}, bf16[16,768]{1,0:T(8,128)(2,1)S(1)}, u32[]{:S(2)}, u32[]{:S(2)}) collective-permute-start(bf16[16,768]{1,0:T(8,128)(2,1)S(1)} %get-tuple-element.46), channel_id=1, source_target_pairs={{0,4},{2,6},{4,0},{6,2},{1,5},{3,7},{5,1},{7,3},{8,12},{10,14},{12... | collective-permute-start | bytes 73736 | tf_op jit(solution)/shard_map/ppermute | solution.py:33
  8.0 18.1 %collective-permute-start.6 = (bf16[16,768]{1,0:T(8,128)(2,1)S(1)}, bf16[16,768]{1,0:T(8,128)(2,1)S(1)}, u32[]{:S(2)}, u32[]{:S(2)}) collective-permute-start(bf16[16,768]{1,0:T(8,128)(2,1)S(1)} %get-tuple-element.46), channel_id=1, source_target_pairs={{0,6},{2,0},{4,2},{6,4},{1,7},{3,1},{5,3},{7,5},{8,14},{10,8},{12,... | collective-permute-start | bytes 73736 | tf_op jit(solution)/shard_map/ppermute | solution.py:33
  11.6 48.2 %collective-permute-start.3 = (bf16[192,768]{1,0:T(8,128)(2,1)S(1)}, bf16[192,768]{1,0:T(8,128)(2,1)S(1)}, u32[]{:S(2)}, u32[]{:S(2)}) collective-permute-start(bf16[192,768]{1,0:T(8,128)(2,1)S(1)} %fusion.10.refs_0_), channel_id=1, source_target_pairs={{2,0},{4,2},{6,4},{3,1},{5,3},{7,5},{10,8},{12,10},{14,12},{11,9},... | collective-permute-start | bytes 884744 | tf_op jit(solution)/shard_map/ppermute | solution.py:28
  12.9 46.9 %collective-permute-start.2 = (bf16[192,768]{1,0:T(8,128)(2,1)S(1)}, bf16[192,768]{1,0:T(8,128)(2,1)S(1)}, u32[]{:S(2)}, u32[]{:S(2)}) collective-permute-start(bf16[192,768]{1,0:T(8,128)(2,1)S(1)} %fusion.10.refs_0_), channel_id=1, source_target_pairs={{0,2},{2,4},{4,6},{1,3},{3,5},{5,7},{8,10},{10,12},{12,14},{9,11},... | collective-permute-start | bytes 884744 | tf_op jit(solution)/shard_map/ppermute | solution.py:28
  26.1 11.5 %collective-permute-start.1 = (bf16[192,768]{1,0:T(8,128)(2,1)S(1)}, bf16[192,768]{1,0:T(8,128)(2,1)S(1)}, u32[]{:S(2)}, u32[]{:S(2)}) collective-permute-start(bf16[192,768]{1,0:T(8,128)(2,1)S(1)} %fusion.10.refs_0_), channel_id=1, source_target_pairs={{8,0},{16,8},{24,16},{9,1},{17,9},{25,17},{10,2},{18,10},{26,18},{... | collective-permute-start | bytes 884744 | tf_op jit(solution)/shard_map/ppermute | solution.py:28
  38.4 22.1 %collective-permute-start.5 = (bf16[384,768]{1,0:T(8,128)(2,1)}, bf16[384,768]{1,0:T(8,128)(2,1)S(1)}, u32[]{:S(2)}, u32[]{:S(2)}) collective-permute-start(bf16[384,768]{1,0:T(8,128)(2,1)} %constant_dynamic-update-slice_fusion), channel_id=1, source_target_pairs={{2,0},{4,2},{6,4},{3,1},{5,3},{7,5},{10,8},{12,10},{14,12},{11,9},... | collective-permute-start | bytes 1769480 | tf_op jit(solution)/shard_map/ppermute | solution.py:28
  39.7 20.8 %collective-permute-start.4 = (bf16[384,768]{1,0:T(8,128)(2,1)}, bf16[384,768]{1,0:T(8,128)(2,1)}, u32[]{:S(2)}, u32[]{:S(2)}) collective-permute-start(bf16[384,768]{1,0:T(8,128)(2,1)} %constant_dynamic-update-slice_fusion), channel_id=1, source_target_pairs={{0,2},{2,4},{4,6},{1,3},{3,5},{5,7},{8,10},{10,12},{12,14},{9,11},... | collective-permute-start | bytes 1769480 | tf_op jit(solution)/shard_map/ppermute | solution.py:28
  99.4 25.7 %collective-permute-start.18 = (bf16[384,768]{1,0:T(8,128)(2,1)}, bf16[384,768]{1,0:T(8,128)(2,1)}, u32[]{:S(2)}, u32[]{:S(2)}) collective-permute-start(bf16[384,768]{1,0:T(8,128)(2,1)} %constant_dynamic-slice_fusion.29), channel_id=1, source_target_pairs={{0,16},{8,24},{16,0},{24,8},{1,17},{9,25},{17,1},{25,9},{2,18},{10... | collective-permute-start | bytes 1769480 | tf_op jit(solution)/shard_map/ppermute | solution.py:38
  103.3 25.4 %collective-permute-start.15 = (bf16[384,768]{1,0:T(8,128)(2,1)}, bf16[384,768]{1,0:T(8,128)(2,1)}, u32[]{:S(2)}, u32[]{:S(2)}) collective-permute-start(bf16[384,768]{1,0:T(8,128)(2,1)} %constant_dynamic-slice_fusion.32), channel_id=1, source_target_pairs={{0,8},{8,0},{16,24},{24,16},{1,9},{9,1},{17,25},{25,17},{2,10},{10... | collective-permute-start | bytes 1769480 | tf_op jit(solution)/shard_map/ppermute | solution.py:38
  106.8 97.5 %collective-permute-start.11 = (bf16[192,768]{1,0:T(8,128)(2,1)S(1)}, bf16[192,768]{1,0:T(8,128)(2,1)S(1)}, u32[]{:S(2)}, u32[]{:S(2)}) collective-permute-start(bf16[192,768]{1,0:T(8,128)(2,1)S(1)} %copy-done.12), channel_id=1, source_target_pairs={{0,2},{2,4},{4,6},{1,3},{3,5},{5,7},{8,10},{10,12},{12,14},{9,11},... | collective-permute-start | bytes 884744 | tf_op jit(solution)/shard_map/ppermute | solution.py:28
  121.7 16.9 %collective-permute-start.13 = (bf16[384,768]{1,0:T(8,128)(2,1)S(1)}, bf16[384,768]{1,0:T(8,128)(2,1)S(1)}, u32[]{:S(2)}, u32[]{:S(2)}) collective-permute-start(bf16[384,768]{1,0:T(8,128)(2,1)S(1)} %copy-done.8), channel_id=1, source_target_pairs={{0,2},{2,4},{4,6},{1,3},{3,5},{5,7},{8,10},{10,12},{12,14},{9,11},... | collective-permute-start | bytes 1769480 | tf_op jit(solution)/shard_map/ppermute | solution.py:28
  123.7 18.9 %collective-permute-start.14 = (bf16[384,768]{1,0:T(8,128)(2,1)S(1)}, bf16[384,768]{1,0:T(8,128)(2,1)S(1)}, u32[]{:S(2)}, u32[]{:S(2)}) collective-permute-start(bf16[384,768]{1,0:T(8,128)(2,1)S(1)} %copy-done.6), channel_id=1, source_target_pairs={{2,0},{4,2},{6,4},{3,1},{5,3},{7,5},{10,8},{12,10},{14,12},{11,9},... | collective-permute-start | bytes 1769480 | tf_op jit(solution)/shard_map/ppermute | solution.py:28
  126.5 16.2 %collective-permute-start.27 = (bf16[192,768]{1,0:T(8,128)(2,1)S(1)}, bf16[192,768]{1,0:T(8,128)(2,1)S(1)}, u32[]{:S(2)}, u32[]{:S(2)}) collective-permute-start(bf16[192,768]{1,0:T(8,128)(2,1)S(1)} %constant_dynamic-slice_fusion.10), channel_id=1, source_target_pairs={{0,8},{8,0},{16,24},{24,16},{1,9},{9,1},{17,25},{25,17},{2,10},{10... | collective-permute-start | bytes 884744 | tf_op jit(solution)/shard_map/ppermute | solution.py:38
  129.9 13.1 %collective-permute-start.26 = (bf16[192,768]{1,0:T(8,128)(2,1)S(1)}, bf16[192,768]{1,0:T(8,128)(2,1)S(1)}, u32[]{:S(2)}, u32[]{:S(2)}) collective-permute-start(bf16[192,768]{1,0:T(8,128)(2,1)S(1)} %constant_dynamic-slice_fusion.12), channel_id=1, source_target_pairs={{0,16},{8,24},{16,0},{24,8},{1,17},{9,25},{17,1},{25,9},{2,18},{10... | collective-permute-start | bytes 884744 | tf_op jit(solution)/shard_map/ppermute | solution.py:38
  138.6 18.4 %collective-permute-start.16 = (bf16[384,768]{1,0:T(8,128)(2,1)S(1)}, bf16[384,768]{1,0:T(8,128)(2,1)S(1)}, u32[]{:S(2)}, u32[]{:S(2)}) collective-permute-start(bf16[384,768]{1,0:T(8,128)(2,1)S(1)} %constant_dynamic-slice_fusion.31), channel_id=1, source_target_pairs={{0,8},{8,0},{16,24},{24,16},{1,9},{9,1},{17,25},{25,17},{2,10},{10... | collective-permute-start | bytes 1769480 | tf_op jit(solution)/shard_map/ppermute | solution.py:38
  151.7 54.1 %collective-permute-start.12 = (bf16[192,768]{1,0:T(8,128)(2,1)S(1)}, bf16[192,768]{1,0:T(8,128)(2,1)S(1)}, u32[]{:S(2)}, u32[]{:S(2)}) collective-permute-start(bf16[192,768]{1,0:T(8,128)(2,1)S(1)} %copy-done.10), channel_id=1, source_target_pairs={{2,0},{4,2},{6,4},{3,1},{5,3},{7,5},{10,8},{12,10},{14,12},{11,9},... | collective-permute-start | bytes 884744 | tf_op jit(solution)/shard_map/ppermute | solution.py:28
  154.7 21.0 %collective-permute-start.19 = (bf16[512,768]{1,0:T(8,128)(2,1)S(1)}, bf16[512,768]{1,0:T(8,128)(2,1)S(1)}, u32[]{:S(2)}, u32[]{:S(2)}) collective-permute-start(bf16[512,768]{1,0:T(8,128)(2,1)S(1)} %pad_maximum_fusion), channel_id=1, source_target_pairs={{0,16},{8,24},{16,0},{24,8},{1,17},{9,25},{17,1},{25,9},{2,18},{10... | collective-permute-start | bytes 2359304 | tf_op jit(solution)/shard_map/ppermute | solution.py:38
  154.9 20.8 %collective-permute-start.33 = (bf16[96,768]{1,0:T(8,128)(2,1)S(1)}, bf16[96,768]{1,0:T(8,128)(2,1)S(1)}, u32[]{:S(2)}, u32[]{:S(2)}) collective-permute-start(bf16[96,768]{1,0:T(8,128)(2,1)S(1)} %get-tuple-element.42), channel_id=1, source_target_pairs={{0,2},{2,4},{4,6},{6,0},{1,3},{3,5},{5,7},{7,1},{8,10},{10,12},{12... | collective-permute-start | bytes 442376 | tf_op jit(solution)/shard_map/ppermute | solution.py:33
  162.9 12.7 %collective-permute-start.32 = (bf16[96,768]{1,0:T(8,128)(2,1)S(1)}, bf16[96,768]{1,0:T(8,128)(2,1)S(1)}, u32[]{:S(2)}, u32[]{:S(2)}) collective-permute-start(bf16[96,768]{1,0:T(8,128)(2,1)S(1)} %get-tuple-element.42), channel_id=1, source_target_pairs={{0,4},{2,6},{4,0},{6,2},{1,5},{3,7},{5,1},{7,3},{8,12},{10,14},{12... | collective-permute-start | bytes 442376 | tf_op jit(solution)/shard_map/ppermute | solution.py:33
  176.1 10.9 %collective-permute-start.20 = (bf16[256,768]{1,0:T(8,128)(2,1)S(1)}, bf16[256,768]{1,0:T(8,128)(2,1)S(1)}, u32[]{:S(2)}, u32[]{:S(2)}) collective-permute-start(bf16[256,768]{1,0:T(8,128)(2,1)S(1)} %pad_maximum_fusion.1), channel_id=1, source_target_pairs={{0,8},{8,0},{16,24},{24,16},{1,9},{9,1},{17,25},{25,17},{2,10},{10... | collective-permute-start | bytes 1179656 | tf_op jit(solution)/shard_map/ppermute | solution.py:38
  188.4 10.0 %collective-permute-start.24 = (bf16[112,768]{1,0:T(8,128)(2,1)S(1)}, bf16[112,768]{1,0:T(8,128)(2,1)S(1)}, u32[]{:S(2)}, u32[]{:S(2)}) collective-permute-start(bf16[112,768]{1,0:T(8,128)(2,1)S(1)} %pad_maximum_fusion.3), channel_id=1, source_target_pairs={{0,4},{2,6},{4,0},{6,2},{1,5},{3,7},{5,1},{7,3},{8,12},{10,14},{12... | collective-permute-start | bytes 516104 | tf_op jit(solution)/shard_map/ppermute | solution.py:33
  194.7 11.1 %collective-permute-start.21 = (bf16[192,768]{1,0:T(8,128)(2,1)S(1)}, bf16[192,768]{1,0:T(8,128)(2,1)S(1)}, u32[]{:S(2)}, u32[]{:S(2)}) collective-permute-start(bf16[192,768]{1,0:T(8,128)(2,1)S(1)} %get-tuple-element.53), channel_id=1, source_target_pairs={{0,8},{8,16},{16,24},{1,9},{9,17},{17,25},{2,10},{10,18},{18,26},{... | collective-permute-start | bytes 884744 | tf_op jit(solution)/shard_map/ppermute | solution.py:28
  198.4 16.8 %collective-permute-start.22 = (bf16[192,768]{1,0:T(8,128)(2,1)S(1)}, bf16[192,768]{1,0:T(8,128)(2,1)S(1)}, u32[]{:S(2)}, u32[]{:S(2)}) collective-permute-start(bf16[192,768]{1,0:T(8,128)(2,1)S(1)} %get-tuple-element.54), channel_id=1, source_target_pairs={{8,0},{16,8},{24,16},{9,1},{17,9},{25,17},{10,2},{18,10},{26,18},{... | collective-permute-start | bytes 884744 | tf_op jit(solution)/shard_map/ppermute | solution.py:28
  199.7 25.0 %collective-permute-start.43 = (bf16[192,768]{1,0:T(8,128)(2,1)S(1)}, bf16[192,768]{1,0:T(8,128)(2,1)S(1)}, u32[]{:S(2)}, u32[]{:S(2)}) collective-permute-start(bf16[192,768]{1,0:T(8,128)(2,1)S(1)} %bitcast.91), channel_id=1, source_target_pairs={{0,8},{8,0},{16,24},{24,16},{1,9},{9,1},{17,25},{25,17},{2,10},{10... | collective-permute-start | bytes 884744 | tf_op jit(solution)/shard_map/ppermute | solution.py:38
  204.3 18.4 %collective-permute-start.34 = (bf16[192,768]{1,0:T(8,128)(2,1)S(1)}, bf16[192,768]{1,0:T(8,128)(2,1)S(1)}, u32[]{:S(2)}, u32[]{:S(2)}) collective-permute-start(bf16[192,768]{1,0:T(8,128)(2,1)S(1)} %bitcast.93), channel_id=1, source_target_pairs={{0,16},{8,24},{16,0},{24,8},{1,17},{9,25},{17,1},{25,9},{2,18},{10... | collective-permute-start | bytes 884744 | tf_op jit(solution)/shard_map/ppermute | solution.py:38
  205.8 9.7 %collective-permute-start.37 = (bf16[96,768]{1,0:T(8,128)(2,1)S(1)}, bf16[96,768]{1,0:T(8,128)(2,1)S(1)}, u32[]{:S(2)}, u32[]{:S(2)}) collective-permute-start(bf16[96,768]{1,0:T(8,128)(2,1)S(1)} %get-tuple-element.40), channel_id=1, source_target_pairs={{0,4},{2,6},{4,0},{6,2},{1,5},{3,7},{5,1},{7,3},{8,12},{10,14},{12... | collective-permute-start | bytes 442376 | tf_op jit(solution)/shard_map/ppermute | solution.py:33
  205.8 9.6 %collective-permute-start.36 = (bf16[96,768]{1,0:T(8,128)(2,1)S(1)}, bf16[96,768]{1,0:T(8,128)(2,1)S(1)}, u32[]{:S(2)}, u32[]{:S(2)}) collective-permute-start(bf16[96,768]{1,0:T(8,128)(2,1)S(1)} %get-tuple-element.40), channel_id=1, source_target_pairs={{0,6},{2,0},{4,2},{6,4},{1,7},{3,1},{5,3},{7,5},{8,14},{10,8},{12,... | collective-permute-start | bytes 442376 | tf_op jit(solution)/shard_map/ppermute | solution.py:33
  222.9 12.5 %collective-permute-start.35 = (bf16[384,768]{1,0:T(8,128)(2,1)S(1)}, bf16[384,768]{1,0:T(8,128)(2,1)S(1)}, u32[]{:S(2)}, u32[]{:S(2)}) collective-permute-start(bf16[384,768]{1,0:T(8,128)(2,1)S(1)} %maximum_select_fusion.4), channel_id=1, source_target_pairs={{0,8},{8,0},{16,24},{24,16},{1,9},{9,1},{17,25},{25,17},{2,10},{10... | collective-permute-start | bytes 1769480 | tf_op jit(solution)/shard_map/ppermute | solution.py:38
  224.9 11.0 %collective-permute-start.44 = (bf16[384,768]{1,0:T(8,128)(2,1)S(1)}, bf16[384,768]{1,0:T(8,128)(2,1)S(1)}, u32[]{:S(2)}, u32[]{:S(2)}) collective-permute-start(bf16[384,768]{1,0:T(8,128)(2,1)S(1)} %maximum_select_fusion.7), channel_id=1, source_target_pairs={{0,16},{8,24},{16,0},{24,8},{1,17},{9,25},{17,1},{25,9},{2,18},{10... | collective-permute-start | bytes 1769480 | tf_op jit(solution)/shard_map/ppermute | solution.py:38
  229.2 12.5 %collective-permute-start.40 = (bf16[384,768]{1,0:T(8,128)(2,1)S(1)}, bf16[384,768]{1,0:T(8,128)(2,1)S(1)}, u32[]{:S(2)}, u32[]{:S(2)}) collective-permute-start(bf16[384,768]{1,0:T(8,128)(2,1)S(1)} %maximum_select_fusion.5), channel_id=1, source_target_pairs={{0,8},{8,0},{16,24},{24,16},{1,9},{9,1},{17,25},{25,17},{2,10},{10... | collective-permute-start | bytes 1769480 | tf_op jit(solution)/shard_map/ppermute | solution.py:38
  229.8 12.4 %collective-permute-start.42 = (bf16[384,768]{1,0:T(8,128)(2,1)S(1)}, bf16[384,768]{1,0:T(8,128)(2,1)S(1)}, u32[]{:S(2)}, u32[]{:S(2)}) collective-permute-start(bf16[384,768]{1,0:T(8,128)(2,1)S(1)} %maximum_select_fusion.6), channel_id=1, source_target_pairs={{0,16},{8,24},{16,0},{24,8},{1,17},{9,25},{17,1},{25,9},{2,18},{10... | collective-permute-start | bytes 1769480 | tf_op jit(solution)/shard_map/ppermute | solution.py:38
  (39 other events, 262.1 us)

commit v2 on v1

--- a/solution.py
+++ b/solution.py
@@ -358,19 +358,20 @@
     for k in range(1, n_tx):
         columns.append(rotated(summary_hidden, "tx", k))
     both = jnp.concatenate([up, down], axis=0)
-    left_two = shifted(both, "tx", 1)
-    right_two = shifted(both, "tx", -1)
     each = summary.shape[0]
     every_summary = in_order(columns, col).reshape(n_tx * each, width)
     for b in bits:
         every_summary = unfold(every_summary, "ty", b, row)
 
+    own, grads_in, counts, both = lax.optimization_barrier((hidden, grads, counts, both))
+    left_two = shifted(both, "tx", 1)
+    right_two = shifted(both, "tx", -1)
     live = jnp.arange(tile, dtype=jnp.int32)[:, None] < lax.dynamic_slice(
         counts, (row, col), (1, 1)
     )
-    masked = jnp.where(live, grads, jnp.zeros_like(grads))
+    masked = jnp.where(live, grads_in, jnp.zeros_like(grads_in))
     factor = 1.0 / math.sqrt(width // HEADS)
-    query = (mm(hidden, projections[0]).astype(bf16) * factor).astype(bf16)
+    query = (mm(own, projections[0]).astype(bf16) * factor).astype(bf16)
     grad = mm(masked, projections[3], ((1,), (1,))).astype(bf16)
     near_counts = lax.dynamic_slice(jnp.pad(counts, 1), (row, col), (3, 3)).reshape(9)
     flags = lax.dynamic_slice(tile_pattern, (row, col, zero), (1, 1, 9)).reshape(9)

time: 250 us -> 240 us (0.960)
  local copies, waits for them, and re-layouts: 20 us -> 13.6 us
  starting transfers between devices: 99.7 us -> 96.6 us
    ppermute x18, waiting for transfers between devices: 25.5 us -> 30.8 us  [swapped(): return lax.ppermute(array, axis, [(i, i ^ 1 << bit) for i in range(peers)])]
    ppermute x12, waiting for transfers between devices: 23 us -> 17.9 us  [shifted(): return lax.ppermute(array, axis, pairs)]
    unnamed x72 -> x63, local copies, waits for them, and re-layouts: 12.6 us -> 7.61 us
    ppermute x18, starting transfers between devices: 28.6 us -> 25.7 us  [swapped(): return lax.ppermute(array, axis, [(i, i ^ 1 << bit) for i in range(peers)])]
  transfers between devices with their start and end apart: 45 -> 45, of which waited for: 19 -> 17; matrix products, arithmetic and copies ran while one was open for 10% -> 9% of each run, Pallas kernels for 0% -> 0%
where the time goes in v2:
time: 240 us; the launch traced here: 239 us
  starting transfers between devices  96.6 us (40%)
  waiting for transfers between devices  74.4 us (31%)
  Pallas kernels  29.9 us (12%)
  other arithmetic  18.7 us (8%)
  local copies, waits for them, and re-layouts  13.6 us (6%)
  matrix products  3.54 us (1%)
    ppermute x12, starting transfers between devices, shifted(): return lax.ppermute(array, axis, pairs)  41.3 us
    ppermute x18, waiting for transfers between devices, swapped(): return lax.ppermute(array, axis, [(i, i ^ 1 << bit) for i in range(peers)])  30.8 us
    pallas_call x1, Pallas kernels, layer(): pl.pallas_call(functools.partial(layer_kernel, segments, len(sources)), i...  29.9 us
    ppermute x15, starting transfers between devices, rotated(): lax.ppermute(array, axis, [(i, (i + by) % peers) for i in range(peers)])  29.6 us
    ppermute x15, waiting for transfers between devices, rotated(): lax.ppermute(array, axis, [(i, (i + by) % peers) for i in range(peers)])  25.8 us
    ppermute x18, starting transfers between devices, swapped(): return lax.ppermute(array, axis, [(i, i ^ 1 << bit) for i in range(peers)])  25.7 us
    ppermute x12, waiting for transfers between devices, shifted(): return lax.ppermute(array, axis, pairs)  17.9 us
    unnamed x63, local copies, waits for them, and re-layouts  7.61 us
  transfers between devices with their start and end apart: 45, of which 17 were waited for; matrix products, arithmetic and copies ran while one was open for 9% of the time, Pallas kernels for 0%

profile of v2, /device:TPU:0, one launch (start us, length us, event | category | flops | bytes accessed | tf_op | source)
XLA Modules:
  0.0 239.0 jit_solution(13843398186776064815)
XLA Ops:
  2.4 3.1 %collective-permute-start.8 = (bf16[16,768]{1,0:T(8,128)(2,1)S(1)}, bf16[16,768]{1,0:T(8,128)(2,1)S(1)}, u32[]{:S(2)}, u32[]{:S(2)}) collective-permute-start(bf16[16,768]{1,0:T(8,128)(2,1)S(1)} %get-tuple-element.54), channel_id=1, source_target_pairs={{0,2},{2,4},{4,6},{6,0},{1,3},{3,5},{5,7},{7,1},{8,10},{10,12},{12... | collective-permute-start | bytes 73736 | tf_op jit(solution)/shard_map/ppermute | solution.py:33
  5.4 2.6 %collective-permute-start.7 = (bf16[16,768]{1,0:T(8,128)(2,1)S(1)}, bf16[16,768]{1,0:T(8,128)(2,1)S(1)}, u32[]{:S(2)}, u32[]{:S(2)}) collective-permute-start(bf16[16,768]{1,0:T(8,128)(2,1)S(1)} %get-tuple-element.54), channel_id=1, source_target_pairs={{0,4},{2,6},{4,0},{6,2},{1,5},{3,7},{5,1},{7,3},{8,12},{10,14},{12... | collective-permute-start | bytes 73736 | tf_op jit(solution)/shard_map/ppermute | solution.py:33
  13.0 4.6 %collective-permute-start.2 = (bf16[192,768]{1,0:T(8,128)(2,1)S(1)}, bf16[192,768]{1,0:T(8,128)(2,1)S(1)}, u32[]{:S(2)}, u32[]{:S(2)}) collective-permute-start(bf16[192,768]{1,0:T(8,128)(2,1)S(1)} %fusion.10.refs_0_), channel_id=1, source_target_pairs={{0,2},{2,4},{4,6},{1,3},{3,5},{5,7},{8,10},{10,12},{12,14},{9,11},... | collective-permute-start | bytes 884744 | tf_op jit(solution)/shard_map/ppermute | solution.py:28
  19.0 4.6 %collective-permute-start = (bf16[192,768]{1,0:T(8,128)(2,1)S(1)}, bf16[192,768]{1,0:T(8,128)(2,1)S(1)}, u32[]{:S(2)}, u32[]{:S(2)}) collective-permute-start(bf16[192,768]{1,0:T(8,128)(2,1)S(1)} %fusion.10.refs_0_), channel_id=1, source_target_pairs={{0,8},{8,16},{16,24},{1,9},{9,17},{17,25},{2,10},{10,18},{18,26},{... | collective-permute-start | bytes 884744 | tf_op jit(solution)/shard_map/ppermute | solution.py:28
  23.7 2.4 %collective-permute-start.9 = (bf16[64,768]{1,0:T(8,128)(2,1)S(1)}, bf16[64,768]{1,0:T(8,128)(2,1)S(1)}, u32[]{:S(2)}, u32[]{:S(2)}) collective-permute-start(bf16[64,768]{1,0:T(8,128)(2,1)S(1)} %bitcast.99), channel_id=1, source_target_pairs={{0,8},{8,0},{16,24},{24,16},{1,9},{9,1},{17,25},{25,17},{2,10},{10... | collective-permute-start | bytes 294920 | tf_op jit(solution)/shard_map/ppermute | solution.py:38
  26.1 9.2 %collective-permute-done.9 = bf16[64,768]{1,0:T(8,128)(2,1)S(1)} collective-permute-done((bf16[64,768]{1,0:T(8,128)(2,1)S(1)}, bf16[64,768]{1,0:T(8,128)(2,1)S(1)}, u32[]{:S(2)}, u32[]{:S(2)}) %collective-permute-start.9) | collective-permute-done | bytes 98336 | tf_op jit(solution)/shard_map/ppermute | solution.py:38
  38.0 5.4 %collective-permute-start.4 = (bf16[384,768]{1,0:T(8,128)(2,1)}, bf16[384,768]{1,0:T(8,128)(2,1)}, u32[]{:S(2)}, u32[]{:S(2)}) collective-permute-start(bf16[384,768]{1,0:T(8,128)(2,1)} %pad_maximum_fusion.1), channel_id=1, source_target_pairs={{0,2},{2,4},{4,6},{1,3},{3,5},{5,7},{8,10},{10,12},{12,14},{9,11},... | collective-permute-start | bytes 1769480 | tf_op jit(solution)/shard_map/ppermute | solution.py:28
  52.9 29.9 %layer.1 = (bf16[192,768]{1,0:T(8,128)(2,1)}, bf16[768,768]{1,0:T(8,128)(2,1)}, bf16[768,768]{1,0:T(8,128)(2,1)}, bf16[768,768]{1,0:T(8,128)(2,1)}, bf16[768,768...) custom-call(s32[2,12]{1,0:T(2,128)S(1)} %pad_add_fusion.meta, ...), custom_call_target="tpu_custom_call" | custom-call | tf_op jit(solution)/shard_map/layer/pallas_call | solution.py:258
  91.5 4.9 %collective-permute-start.15 = (bf16[384,768]{1,0:T(8,128)(2,1)}, bf16[384,768]{1,0:T(8,128)(2,1)}, u32[]{:S(2)}, u32[]{:S(2)}) collective-permute-start(bf16[384,768]{1,0:T(8,128)(2,1)} %constant_dynamic-slice_fusion.32), channel_id=1, source_target_pairs={{0,8},{8,0},{16,24},{24,16},{1,9},{9,1},{17,25},{25,17},{2,10},{10... | collective-permute-start | bytes 1769480 | tf_op jit(solution)/shard_map/ppermute | solution.py:38
  96.4 15.6 %collective-permute-start.11 = (bf16[192,768]{1,0:T(8,128)(2,1)S(1)}, bf16[192,768]{1,0:T(8,128)(2,1)S(1)}, u32[]{:S(2)}, u32[]{:S(2)}) collective-permute-start(bf16[192,768]{1,0:T(8,128)(2,1)S(1)} %copy-done.8), channel_id=1, source_target_pairs={{0,2},{2,4},{4,6},{1,3},{3,5},{5,7},{8,10},{10,12},{12,14},{9,11},... | collective-permute-start | bytes 884744 | tf_op jit(solution)/shard_map/ppermute | solution.py:28
  116.8 2.1 collective-permute-start.27
  120.3 8.6 %collective-permute-done.13 = bf16[384,768]{1,0:T(8,128)(2,1)S(1)} collective-permute-done((bf16[384,768]{1,0:T(8,128)(2,1)S(1)}, bf16[384,768]{1,0:T(8,128)(2,1)S(1)}, u32[]{:S(2)}, u32[]{:S(2)}) %collective-permute-start.13) | collective-permute-done | bytes 589856 | tf_op jit(solution)/shard_map/ppermute | solution.py:28
  132.3 3.0 %collective-permute-start.28 = (bf16[96,768]{1,0:T(8,128)(2,1)S(1)}, bf16[96,768]{1,0:T(8,128)(2,1)S(1)}, u32[]{:S(2)}, u32[]{:S(2)}) collective-permute-start(bf16[96,768]{1,0:T(8,128)(2,1)S(1)} %pad_maximum_fusion.6), channel_id=1, source_target_pairs={{0,2},{2,4},{4,6},{6,0},{1,3},{3,5},{5,7},{7,1},{8,10},{10,12},{12... | collective-permute-start | bytes 442376 | tf_op jit(solution)/shard_map/ppermute | solution.py:33
  135.4 2.4 %collective-permute-start.30 = (bf16[96,768]{1,0:T(8,128)(2,1)S(1)}, bf16[96,768]{1,0:T(8,128)(2,1)S(1)}, u32[]{:S(2)}, u32[]{:S(2)}) collective-permute-start(bf16[96,768]{1,0:T(8,128)(2,1)S(1)} %pad_maximum_fusion.8), channel_id=1, source_target_pairs={{0,6},{2,0},{4,2},{6,4},{1,7},{3,1},{5,3},{7,5},{8,14},{10,8},{12,... | collective-permute-start | bytes 442376 | tf_op jit(solution)/shard_map/ppermute | solution.py:33
  138.0 2.3 collective-permute-done.28
  141.6 2.7 %collective-permute-done.29 = bf16[96,768]{1,0:T(8,128)(2,1)S(1)} collective-permute-done((bf16[96,768]{1,0:T(8,128)(2,1)S(1)}, bf16[96,768]{1,0:T(8,128)(2,1)S(1)}, u32[]{:S(2)}, u32[]{:S(2)}) %collective-permute-start.29) | collective-permute-done | bytes 147488 | tf_op jit(solution)/shard_map/ppermute | solution.py:33
  146.6 3.2 %collective-permute-start.31 = (bf16[96,768]{1,0:T(8,128)(2,1)S(1)}, bf16[96,768]{1,0:T(8,128)(2,1)S(1)}, u32[]{:S(2)}, u32[]{:S(2)}) collective-permute-start(bf16[96,768]{1,0:T(8,128)(2,1)S(1)} %get-tuple-element.50), channel_id=1, source_target_pairs={{0,6},{2,0},{4,2},{6,4},{1,7},{3,1},{5,3},{7,5},{8,14},{10,8},{12,... | collective-permute-start | bytes 442376 | tf_op jit(solution)/shard_map/ppermute | solution.py:33
  150.0 3.4 %collective-permute-done.31 = bf16[96,768]{1,0:T(8,128)(2,1)S(1)} collective-permute-done((bf16[96,768]{1,0:T(8,128)(2,1)S(1)}, bf16[96,768]{1,0:T(8,128)(2,1)S(1)}, u32[]{:S(2)}, u32[]{:S(2)}) %collective-permute-start.31) | collective-permute-done | bytes 147488 | tf_op jit(solution)/shard_map/ppermute | solution.py:33
  153.4 5.8 %collective-permute-start.32 = (bf16[96,768]{1,0:T(8,128)(2,1)S(1)}, bf16[96,768]{1,0:T(8,128)(2,1)S(1)}, u32[]{:S(2)}, u32[]{:S(2)}) collective-permute-start(bf16[96,768]{1,0:T(8,128)(2,1)S(1)} %get-tuple-element.50), channel_id=1, source_target_pairs={{0,4},{2,6},{4,0},{6,2},{1,5},{3,7},{5,1},{7,3},{8,12},{10,14},{12... | collective-permute-start | bytes 442376 | tf_op jit(solution)/shard_map/ppermute | solution.py:33
  159.3 6.1 %collective-permute-done.32 = bf16[96,768]{1,0:T(8,128)(2,1)S(1)} collective-permute-done((bf16[96,768]{1,0:T(8,128)(2,1)S(1)}, bf16[96,768]{1,0:T(8,128)(2,1)S(1)}, u32[]{:S(2)}, u32[]{:S(2)}) %collective-permute-start.32) | collective-permute-done | bytes 147488 | tf_op jit(solution)/shard_map/ppermute | solution.py:33
  166.9 6.6 %collective-permute-done.17 = bf16[192,768]{1,0:T(8,128)(2,1)S(1)} collective-permute-done((bf16[192,768]{1,0:T(8,128)(2,1)S(1)}, bf16[192,768]{1,0:T(8,128)(2,1)S(1)}, u32[]{:S(2)}, u32[]{:S(2)}) %collective-permute-start.17) | collective-permute-done | bytes 294944 | tf_op jit(solution)/shard_map/ppermute | solution.py:38
  173.6 4.2 %collective-permute-done.20 = bf16[256,768]{1,0:T(8,128)(2,1)S(1)} collective-permute-done((bf16[256,768]{1,0:T(8,128)(2,1)S(1)}, bf16[256,768]{1,0:T(8,128)(2,1)S(1)}, u32[]{:S(2)}, u32[]{:S(2)}) %collective-permute-start.20) | collective-permute-done | bytes 393248 | tf_op jit(solution)/shard_map/ppermute | solution.py:38
  178.1 2.8 %collective-permute-start.24 = (bf16[112,768]{1,0:T(8,128)(2,1)S(1)}, bf16[112,768]{1,0:T(8,128)(2,1)S(1)}, u32[]{:S(2)}, u32[]{:S(2)}) collective-permute-start(bf16[112,768]{1,0:T(8,128)(2,1)S(1)} %pad_maximum_fusion.4), channel_id=1, source_target_pairs={{0,4},{2,6},{4,0},{6,2},{1,5},{3,7},{5,1},{7,3},{8,12},{10,14},{12... | collective-permute-start | bytes 516104 | tf_op jit(solution)/shard_map/ppermute | solution.py:33
  182.2 3.3 %collective-permute-done.23 = bf16[112,768]{1,0:T(8,128)(2,1)S(1)} collective-permute-done((bf16[112,768]{1,0:T(8,128)(2,1)S(1)}, bf16[112,768]{1,0:T(8,128)(2,1)S(1)}, u32[]{:S(2)}, u32[]{:S(2)}) %collective-permute-start.23) | collective-permute-done | bytes 172064 | tf_op jit(solution)/shard_map/ppermute | solution.py:33
  189.5 3.5 %collective-permute-start.43 = (bf16[192,768]{1,0:T(8,128)(2,1)S(1)}, bf16[192,768]{1,0:T(8,128)(2,1)S(1)}, u32[]{:S(2)}, u32[]{:S(2)}) collective-permute-start(bf16[192,768]{1,0:T(8,128)(2,1)S(1)} %bitcast.87), channel_id=1, source_target_pairs={{0,8},{8,0},{16,24},{24,16},{1,9},{9,1},{17,25},{25,17},{2,10},{10... | collective-permute-start | bytes 884744 | tf_op jit(solution)/shard_map/ppermute | solution.py:38
  195.5 2.7 %collective-permute-start.36 = (bf16[96,768]{1,0:T(8,128)(2,1)S(1)}, bf16[96,768]{1,0:T(8,128)(2,1)S(1)}, u32[]{:S(2)}, u32[]{:S(2)}) collective-permute-start(bf16[96,768]{1,0:T(8,128)(2,1)S(1)} %get-tuple-element.48), channel_id=1, source_target_pairs={{0,6},{2,0},{4,2},{6,4},{1,7},{3,1},{5,3},{7,5},{8,14},{10,8},{12,... | collective-permute-start | bytes 442376 | tf_op jit(solution)/shard_map/ppermute | solution.py:33
  198.3 6.9 %collective-permute-done.22 = bf16[192,768]{1,0:T(8,128)(2,1)S(1)} collective-permute-done((bf16[192,768]{1,0:T(8,128)(2,1)S(1)}, bf16[192,768]{1,0:T(8,128)(2,1)S(1)}, u32[]{:S(2)}, u32[]{:S(2)}) %collective-permute-start.22) | collective-permute-done | bytes 294944 | tf_op jit(solution)/shard_map/ppermute | solution.py:28
  205.6 6.5 %collective-permute-done.38 = bf16[96,768]{1,0:T(8,128)(2,1)S(1)} collective-permute-done((bf16[96,768]{1,0:T(8,128)(2,1)S(1)}, bf16[96,768]{1,0:T(8,128)(2,1)S(1)}, u32[]{:S(2)}, u32[]{:S(2)}) %collective-permute-start.38) | collective-permute-done | bytes 147488 | tf_op jit(solution)/shard_map/ppermute | solution.py:33
  216.9 2.1 collective-permute-done.39
  222.3 3.2 %collective-permute-done.35 = bf16[384,768]{1,0:T(8,128)(2,1)S(1)} collective-permute-done((bf16[384,768]{1,0:T(8,128)(2,1)S(1)}, bf16[384,768]{1,0:T(8,128)(2,1)S(1)}, u32[]{:S(2)}, u32[]{:S(2)}) %collective-permute-start.35) | collective-permute-done | bytes 589856 | tf_op jit(solution)/shard_map/ppermute | solution.py:38
  226.4 5.4 %collective-permute-done.40 = bf16[384,768]{1,0:T(8,128)(2,1)S(1)} collective-permute-done((bf16[384,768]{1,0:T(8,128)(2,1)S(1)}, bf16[384,768]{1,0:T(8,128)(2,1)S(1)}, u32[]{:S(2)}, u32[]{:S(2)}) %collective-permute-start.40) | collective-permute-done | bytes 589856 | tf_op jit(solution)/shard_map/ppermute | solution.py:38
  235.4 3.0 %copy-done.9 = f32[4,768,768]{2,1,0:T(8,128)} copy-done((f32[4,768,768]{2,1,0:T(8,128)}, f32[4,768,768]{2,1,0:T(8,128)S(1)}, u32[]{:S(2)}) %copy-start.9) | copy-done | bytes 9437208
  (206 shorter events, 64.5 us)
Async XLA Ops:
  2.4 21.2 %collective-permute-start.8 = (bf16[16,768]{1,0:T(8,128)(2,1)S(1)}, bf16[16,768]{1,0:T(8,128)(2,1)S(1)}, u32[]{:S(2)}, u32[]{:S(2)}) collective-permute-start(bf16[16,768]{1,0:T(8,128)(2,1)S(1)} %get-tuple-element.54), channel_id=1, source_target_pairs={{0,2},{2,4},{4,6},{6,0},{1,3},{3,5},{5,7},{7,1},{8,10},{10,12},{12... | collective-permute-start | bytes 73736 | tf_op jit(solution)/shard_map/ppermute | solution.py:33
  5.4 13.5 %collective-permute-start.7 = (bf16[16,768]{1,0:T(8,128)(2,1)S(1)}, bf16[16,768]{1,0:T(8,128)(2,1)S(1)}, u32[]{:S(2)}, u32[]{:S(2)}) collective-permute-start(bf16[16,768]{1,0:T(8,128)(2,1)S(1)} %get-tuple-element.54), channel_id=1, source_target_pairs={{0,4},{2,6},{4,0},{6,2},{1,5},{3,7},{5,1},{7,3},{8,12},{10,14},{12... | collective-permute-start | bytes 73736 | tf_op jit(solution)/shard_map/ppermute | solution.py:33
  11.6 40.4 %collective-permute-start.3 = (bf16[192,768]{1,0:T(8,128)(2,1)S(1)}, bf16[192,768]{1,0:T(8,128)(2,1)S(1)}, u32[]{:S(2)}, u32[]{:S(2)}) collective-permute-start(bf16[192,768]{1,0:T(8,128)(2,1)S(1)} %fusion.10.refs_0_), channel_id=1, source_target_pairs={{2,0},{4,2},{6,4},{3,1},{5,3},{7,5},{10,8},{12,10},{14,12},{11,9},... | collective-permute-start | bytes 884744 | tf_op jit(solution)/shard_map/ppermute | solution.py:28
  13.0 39.0 %collective-permute-start.2 = (bf16[192,768]{1,0:T(8,128)(2,1)S(1)}, bf16[192,768]{1,0:T(8,128)(2,1)S(1)}, u32[]{:S(2)}, u32[]{:S(2)}) collective-permute-start(bf16[192,768]{1,0:T(8,128)(2,1)S(1)} %fusion.10.refs_0_), channel_id=1, source_target_pairs={{0,2},{2,4},{4,6},{1,3},{3,5},{5,7},{8,10},{10,12},{12,14},{9,11},... | collective-permute-start | bytes 884744 | tf_op jit(solution)/shard_map/ppermute | solution.py:28
  17.7 18.2 %collective-permute-start.1 = (bf16[192,768]{1,0:T(8,128)(2,1)S(1)}, bf16[192,768]{1,0:T(8,128)(2,1)S(1)}, u32[]{:S(2)}, u32[]{:S(2)}) collective-permute-start(bf16[192,768]{1,0:T(8,128)(2,1)S(1)} %fusion.10.refs_0_), channel_id=1, source_target_pairs={{8,0},{16,8},{24,16},{9,1},{17,9},{25,17},{10,2},{18,10},{26,18},{... | collective-permute-start | bytes 884744 | tf_op jit(solution)/shard_map/ppermute | solution.py:28
  19.0 16.9 %collective-permute-start = (bf16[192,768]{1,0:T(8,128)(2,1)S(1)}, bf16[192,768]{1,0:T(8,128)(2,1)S(1)}, u32[]{:S(2)}, u32[]{:S(2)}) collective-permute-start(bf16[192,768]{1,0:T(8,128)(2,1)S(1)} %fusion.10.refs_0_), channel_id=1, source_target_pairs={{0,8},{8,16},{16,24},{1,9},{9,17},{17,25},{2,10},{10,18},{18,26},{... | collective-permute-start | bytes 884744 | tf_op jit(solution)/shard_map/ppermute | solution.py:28
  23.7 11.7 %collective-permute-start.9 = (bf16[64,768]{1,0:T(8,128)(2,1)S(1)}, bf16[64,768]{1,0:T(8,128)(2,1)S(1)}, u32[]{:S(2)}, u32[]{:S(2)}) collective-permute-start(bf16[64,768]{1,0:T(8,128)(2,1)S(1)} %bitcast.99), channel_id=1, source_target_pairs={{0,8},{8,0},{16,24},{24,16},{1,9},{9,1},{17,25},{25,17},{2,10},{10... | collective-permute-start | bytes 294920 | tf_op jit(solution)/shard_map/ppermute | solution.py:38
  35.4 16.5 %collective-permute-start.10 = (bf16[128,768]{1,0:T(8,128)(2,1)S(1)}, bf16[128,768]{1,0:T(8,128)(2,1)S(1)}, u32[]{:S(2)}, u32[]{:S(2)}) collective-permute-start(bf16[128,768]{1,0:T(8,128)(2,1)S(1)} %maximum_select_fusion.9), channel_id=1, source_target_pairs={{0,16},{8,24},{16,0},{24,8},{1,17},{9,25},{17,1},{25,9},{2,18},{10... | collective-permute-start | bytes 589832 | tf_op jit(solution)/shard_map/ppermute | solution.py:38
  36.8 15.3 %collective-permute-start.5 = (bf16[384,768]{1,0:T(8,128)(2,1)}, bf16[384,768]{1,0:T(8,128)(2,1)S(1)}, u32[]{:S(2)}, u32[]{:S(2)}) collective-permute-start(bf16[384,768]{1,0:T(8,128)(2,1)} %pad_maximum_fusion.1), channel_id=1, source_target_pairs={{2,0},{4,2},{6,4},{3,1},{5,3},{7,5},{10,8},{12,10},{14,12},{11,9},... | collective-permute-start | bytes 1769480 | tf_op jit(solution)/shard_map/ppermute | solution.py:28
  38.0 14.6 %collective-permute-start.4 = (bf16[384,768]{1,0:T(8,128)(2,1)}, bf16[384,768]{1,0:T(8,128)(2,1)}, u32[]{:S(2)}, u32[]{:S(2)}) collective-permute-start(bf16[384,768]{1,0:T(8,128)(2,1)} %pad_maximum_fusion.1), channel_id=1, source_target_pairs={{0,2},{2,4},{4,6},{1,3},{3,5},{5,7},{8,10},{10,12},{12,14},{9,11},... | collective-permute-start | bytes 1769480 | tf_op jit(solution)/shard_map/ppermute | solution.py:28
  88.0 27.3 %collective-permute-start.18 = (bf16[384,768]{1,0:T(8,128)(2,1)}, bf16[384,768]{1,0:T(8,128)(2,1)}, u32[]{:S(2)}, u32[]{:S(2)}) collective-permute-start(bf16[384,768]{1,0:T(8,128)(2,1)} %constant_dynamic-slice_fusion.29), channel_id=1, source_target_pairs={{0,16},{8,24},{16,0},{24,8},{1,17},{9,25},{17,1},{25,9},{2,18},{10... | collective-permute-start | bytes 1769480 | tf_op jit(solution)/shard_map/ppermute | solution.py:38
  91.5 27.4 %collective-permute-start.15 = (bf16[384,768]{1,0:T(8,128)(2,1)}, bf16[384,768]{1,0:T(8,128)(2,1)}, u32[]{:S(2)}, u32[]{:S(2)}) collective-permute-start(bf16[384,768]{1,0:T(8,128)(2,1)} %constant_dynamic-slice_fusion.32), channel_id=1, source_target_pairs={{0,8},{8,0},{16,24},{24,16},{1,9},{9,1},{17,25},{25,17},{2,10},{10... | collective-permute-start | bytes 1769480 | tf_op jit(solution)/shard_map/ppermute | solution.py:38
  96.4 97.6 %collective-permute-start.11 = (bf16[192,768]{1,0:T(8,128)(2,1)S(1)}, bf16[192,768]{1,0:T(8,128)(2,1)S(1)}, u32[]{:S(2)}, u32[]{:S(2)}) collective-permute-start(bf16[192,768]{1,0:T(8,128)(2,1)S(1)} %copy-done.8), channel_id=1, source_target_pairs={{0,2},{2,4},{4,6},{1,3},{3,5},{5,7},{8,10},{10,12},{12,14},{9,11},... | collective-permute-start | bytes 884744 | tf_op jit(solution)/shard_map/ppermute | solution.py:28
  112.0 16.9 %collective-permute-start.13 = (bf16[384,768]{1,0:T(8,128)(2,1)S(1)}, bf16[384,768]{1,0:T(8,128)(2,1)S(1)}, u32[]{:S(2)}, u32[]{:S(2)}) collective-permute-start(bf16[384,768]{1,0:T(8,128)(2,1)S(1)} %copy-done.4), channel_id=1, source_target_pairs={{0,2},{2,4},{4,6},{1,3},{3,5},{5,7},{8,10},{10,12},{12,14},{9,11},... | collective-permute-start | bytes 1769480 | tf_op jit(solution)/shard_map/ppermute | solution.py:28
  114.0 17.8 %collective-permute-start.14 = (bf16[384,768]{1,0:T(8,128)(2,1)S(1)}, bf16[384,768]{1,0:T(8,128)(2,1)S(1)}, u32[]{:S(2)}, u32[]{:S(2)}) collective-permute-start(bf16[384,768]{1,0:T(8,128)(2,1)S(1)} %copy-done.2), channel_id=1, source_target_pairs={{2,0},{4,2},{6,4},{3,1},{5,3},{7,5},{10,8},{12,10},{14,12},{11,9},... | collective-permute-start | bytes 1769480 | tf_op jit(solution)/shard_map/ppermute | solution.py:28
  116.8 15.2 %collective-permute-start.27 = (bf16[192,768]{1,0:T(8,128)(2,1)S(1)}, bf16[192,768]{1,0:T(8,128)(2,1)S(1)}, u32[]{:S(2)}, u32[]{:S(2)}) collective-permute-start(bf16[192,768]{1,0:T(8,128)(2,1)S(1)} %constant_dynamic-slice_fusion.10), channel_id=1, source_target_pairs={{0,8},{8,0},{16,24},{24,16},{1,9},{9,1},{17,25},{25,17},{2,10},{10... | collective-permute-start | bytes 884744 | tf_op jit(solution)/shard_map/ppermute | solution.py:38
  120.2 12.0 %collective-permute-start.26 = (bf16[192,768]{1,0:T(8,128)(2,1)S(1)}, bf16[192,768]{1,0:T(8,128)(2,1)S(1)}, u32[]{:S(2)}, u32[]{:S(2)}) collective-permute-start(bf16[192,768]{1,0:T(8,128)(2,1)S(1)} %constant_dynamic-slice_fusion.12), channel_id=1, source_target_pairs={{0,16},{8,24},{16,0},{24,8},{1,17},{9,25},{17,1},{25,9},{2,18},{10... | collective-permute-start | bytes 884744 | tf_op jit(solution)/shard_map/ppermute | solution.py:38
  128.9 17.7 %collective-permute-start.16 = (bf16[384,768]{1,0:T(8,128)(2,1)S(1)}, bf16[384,768]{1,0:T(8,128)(2,1)S(1)}, u32[]{:S(2)}, u32[]{:S(2)}) collective-permute-start(bf16[384,768]{1,0:T(8,128)(2,1)S(1)} %constant_dynamic-slice_fusion.31), channel_id=1, source_target_pairs={{0,8},{8,0},{16,24},{24,16},{1,9},{9,1},{17,25},{25,17},{2,10},{10... | collective-permute-start | bytes 1769480 | tf_op jit(solution)/shard_map/ppermute | solution.py:38
  140.3 55.2 %collective-permute-start.12 = (bf16[192,768]{1,0:T(8,128)(2,1)S(1)}, bf16[192,768]{1,0:T(8,128)(2,1)S(1)}, u32[]{:S(2)}, u32[]{:S(2)}) collective-permute-start(bf16[192,768]{1,0:T(8,128)(2,1)S(1)} %copy-done.6), channel_id=1, source_target_pairs={{2,0},{4,2},{6,4},{3,1},{5,3},{7,5},{10,8},{12,10},{14,12},{11,9},... | collective-permute-start | bytes 884744 | tf_op jit(solution)/shard_map/ppermute | solution.py:28
  144.3 21.7 %collective-permute-start.19 = (bf16[512,768]{1,0:T(8,128)(2,1)S(1)}, bf16[512,768]{1,0:T(8,128)(2,1)S(1)}, u32[]{:S(2)}, u32[]{:S(2)}) collective-permute-start(bf16[512,768]{1,0:T(8,128)(2,1)S(1)} %pad_maximum_fusion), channel_id=1, source_target_pairs={{0,16},{8,24},{16,0},{24,8},{1,17},{9,25},{17,1},{25,9},{2,18},{10... | collective-permute-start | bytes 2359304 | tf_op jit(solution)/shard_map/ppermute | solution.py:38
  145.3 20.7 %collective-permute-start.33 = (bf16[96,768]{1,0:T(8,128)(2,1)S(1)}, bf16[96,768]{1,0:T(8,128)(2,1)S(1)}, u32[]{:S(2)}, u32[]{:S(2)}) collective-permute-start(bf16[96,768]{1,0:T(8,128)(2,1)S(1)} %get-tuple-element.50), channel_id=1, source_target_pairs={{0,2},{2,4},{4,6},{6,0},{1,3},{3,5},{5,7},{7,1},{8,10},{10,12},{12... | collective-permute-start | bytes 442376 | tf_op jit(solution)/shard_map/ppermute | solution.py:33
  153.4 12.0 %collective-permute-start.32 = (bf16[96,768]{1,0:T(8,128)(2,1)S(1)}, bf16[96,768]{1,0:T(8,128)(2,1)S(1)}, u32[]{:S(2)}, u32[]{:S(2)}) collective-permute-start(bf16[96,768]{1,0:T(8,128)(2,1)S(1)} %get-tuple-element.50), channel_id=1, source_target_pairs={{0,4},{2,6},{4,0},{6,2},{1,5},{3,7},{5,1},{7,3},{8,12},{10,14},{12... | collective-permute-start | bytes 442376 | tf_op jit(solution)/shard_map/ppermute | solution.py:33
  166.4 11.4 %collective-permute-start.20 = (bf16[256,768]{1,0:T(8,128)(2,1)S(1)}, bf16[256,768]{1,0:T(8,128)(2,1)S(1)}, u32[]{:S(2)}, u32[]{:S(2)}) collective-permute-start(bf16[256,768]{1,0:T(8,128)(2,1)S(1)} %pad_maximum_fusion.2), channel_id=1, source_target_pairs={{0,8},{8,0},{16,24},{24,16},{1,9},{9,1},{17,25},{25,17},{2,10},{10... | collective-permute-start | bytes 1179656 | tf_op jit(solution)/shard_map/ppermute | solution.py:38
  178.1 10.1 %collective-permute-start.24 = (bf16[112,768]{1,0:T(8,128)(2,1)S(1)}, bf16[112,768]{1,0:T(8,128)(2,1)S(1)}, u32[]{:S(2)}, u32[]{:S(2)}) collective-permute-start(bf16[112,768]{1,0:T(8,128)(2,1)S(1)} %pad_maximum_fusion.4), channel_id=1, source_target_pairs={{0,4},{2,6},{4,0},{6,2},{1,5},{3,7},{5,1},{7,3},{8,12},{10,14},{12... | collective-permute-start | bytes 516104 | tf_op jit(solution)/shard_map/ppermute | solution.py:33
  185.5 10.1 %collective-permute-start.21 = (bf16[192,768]{1,0:T(8,128)(2,1)S(1)}, bf16[192,768]{1,0:T(8,128)(2,1)S(1)}, u32[]{:S(2)}, u32[]{:S(2)}) collective-permute-start(bf16[192,768]{1,0:T(8,128)(2,1)S(1)} %get-tuple-element.61), channel_id=1, source_target_pairs={{0,8},{8,16},{16,24},{1,9},{9,17},{17,25},{2,10},{10,18},{18,26},{... | collective-permute-start | bytes 884744 | tf_op jit(solution)/shard_map/ppermute | solution.py:28
  188.2 17.0 %collective-permute-start.22 = (bf16[192,768]{1,0:T(8,128)(2,1)S(1)}, bf16[192,768]{1,0:T(8,128)(2,1)S(1)}, u32[]{:S(2)}, u32[]{:S(2)}) collective-permute-start(bf16[192,768]{1,0:T(8,128)(2,1)S(1)} %get-tuple-element.62), channel_id=1, source_target_pairs={{8,0},{16,8},{24,16},{9,1},{17,9},{25,17},{10,2},{18,10},{26,18},{... | collective-permute-start | bytes 884744 | tf_op jit(solution)/shard_map/ppermute | solution.py:28
  189.5 25.2 %collective-permute-start.43 = (bf16[192,768]{1,0:T(8,128)(2,1)S(1)}, bf16[192,768]{1,0:T(8,128)(2,1)S(1)}, u32[]{:S(2)}, u32[]{:S(2)}) collective-permute-start(bf16[192,768]{1,0:T(8,128)(2,1)S(1)} %bitcast.87), channel_id=1, source_target_pairs={{0,8},{8,0},{16,24},{24,16},{1,9},{9,1},{17,25},{25,17},{2,10},{10... | collective-permute-start | bytes 884744 | tf_op jit(solution)/shard_map/ppermute | solution.py:38
  194.0 18.4 %collective-permute-start.34 = (bf16[192,768]{1,0:T(8,128)(2,1)S(1)}, bf16[192,768]{1,0:T(8,128)(2,1)S(1)}, u32[]{:S(2)}, u32[]{:S(2)}) collective-permute-start(bf16[192,768]{1,0:T(8,128)(2,1)S(1)} %bitcast.89), channel_id=1, source_target_pairs={{0,16},{8,24},{16,0},{24,8},{1,17},{9,25},{17,1},{25,9},{2,18},{10... | collective-permute-start | bytes 884744 | tf_op jit(solution)/shard_map/ppermute | solution.py:38
  212.6 12.8 %collective-permute-start.35 = (bf16[384,768]{1,0:T(8,128)(2,1)S(1)}, bf16[384,768]{1,0:T(8,128)(2,1)S(1)}, u32[]{:S(2)}, u32[]{:S(2)}) collective-permute-start(bf16[384,768]{1,0:T(8,128)(2,1)S(1)} %maximum_select_fusion.4), channel_id=1, source_target_pairs={{0,8},{8,0},{16,24},{24,16},{1,9},{9,1},{17,25},{25,17},{2,10},{10... | collective-permute-start | bytes 1769480 | tf_op jit(solution)/shard_map/ppermute | solution.py:38
  214.9 11.0 %collective-permute-start.44 = (bf16[384,768]{1,0:T(8,128)(2,1)S(1)}, bf16[384,768]{1,0:T(8,128)(2,1)S(1)}, u32[]{:S(2)}, u32[]{:S(2)}) collective-permute-start(bf16[384,768]{1,0:T(8,128)(2,1)S(1)} %maximum_select_fusion.7), channel_id=1, source_target_pairs={{0,16},{8,24},{16,0},{24,8},{1,17},{9,25},{17,1},{25,9},{2,18},{10... | collective-permute-start | bytes 1769480 | tf_op jit(solution)/shard_map/ppermute | solution.py:38
  219.2 12.5 %collective-permute-start.40 = (bf16[384,768]{1,0:T(8,128)(2,1)S(1)}, bf16[384,768]{1,0:T(8,128)(2,1)S(1)}, u32[]{:S(2)}, u32[]{:S(2)}) collective-permute-start(bf16[384,768]{1,0:T(8,128)(2,1)S(1)} %maximum_select_fusion.5), channel_id=1, source_target_pairs={{0,8},{8,0},{16,24},{24,16},{1,9},{9,1},{17,25},{25,17},{2,10},{10... | collective-permute-start | bytes 1769480 | tf_op jit(solution)/shard_map/ppermute | solution.py:38
  219.5 12.7 %collective-permute-start.42 = (bf16[384,768]{1,0:T(8,128)(2,1)S(1)}, bf16[384,768]{1,0:T(8,128)(2,1)S(1)}, u32[]{:S(2)}, u32[]{:S(2)}) collective-permute-start(bf16[384,768]{1,0:T(8,128)(2,1)S(1)} %maximum_select_fusion.6), channel_id=1, source_target_pairs={{0,16},{8,24},{16,0},{24,8},{1,17},{9,25},{17,1},{25,9},{2,18},{10... | collective-permute-start | bytes 1769480 | tf_op jit(solution)/shard_map/ppermute | solution.py:38
  (35 other events, 329.5 us)
